TPU v7x, 32 devices: a whole 2x2x4 slice. The times are simulated.
32 devices in a mesh: rep: 8 (over y, x, core), shard: 4 (over z).
Axes of the slice: x: 2, y: 2, z: 4, core: 2. Of those that a mesh axis runs over, the one named last changes fastest.
Arguments:
- inputs: bfloat16 [16, 1024, 1280], P('rep', 'shard'), may hold values from -6 to 6
- lengths: int32 [16], P('rep'), may hold values from 256 to 1024, as said below
- cotangent: bfloat16 [16, 1024, 1280], P('rep', 'shard'), may hold values from -6 to 6
- attn_gain: bfloat16 [2, 1280], P(None, 'shard'), may hold values from 0.5 to 1.5
- attn_shift: bfloat16 [2, 1280], P(None, 'shard'), may hold values from -1.25 to 1.25
- query_weight: bfloat16 [2, 1280, 1280], P(None, 'shard'), may hold values from -0.15625 to 0.15625
- query_bias: bfloat16 [2, 1280], P(None, 'shard'), may hold values from -1.25 to 1.25
- key_weight: bfloat16 [2, 1280, 1280], P(None, 'shard'), may hold values from -0.15625 to 0.15625
- value_weight: bfloat16 [2, 1280, 1280], P(None, 'shard'), may hold values from -0.15625 to 0.15625
- value_bias: bfloat16 [2, 1280], P(None, 'shard'), may hold values from -1.25 to 1.25
- out_weight: bfloat16 [2, 1280, 1280], P(None, 'shard'), may hold values from -2.5 to 2.5
- out_bias: bfloat16 [2, 1280], P(None, 'shard'), may hold values from -1.25 to 1.25
- mlp_gain: bfloat16 [2, 1280], P(None, 'shard'), may hold values from 0.5 to 1.5
- mlp_shift: bfloat16 [2, 1280], P(None, 'shard'), may hold values from -1.25 to 1.25
- up_weight: bfloat16 [2, 1280, 5120], P(None, 'shard'), may hold values from -0.15625 to 0.15625
- up_bias: bfloat16 [2, 5120], P(None, 'shard'), may hold values from -1.25 to 1.25
- down_weight: bfloat16 [2, 5120, 1280], P(None, 'shard'), may hold values from -0.078125 to 0.078125
- down_bias: bfloat16 [2, 1280], P(None, 'shard'), may hold values from -1.25 to 1.25
Outputs:
- output: bfloat16 [16, 1024, 1280], P('rep', 'shard')
- input_grad: float32 [16, 1024, 1280], P('rep', 'shard')
- attn_gain_grad: float32 [2, 1280], P(None, 'shard')
- attn_shift_grad: float32 [2, 1280], P(None, 'shard')
- query_weight_grad: float32 [2, 1280, 1280], P(None, 'shard')
- query_bias_grad: float32 [2, 1280], P(None, 'shard')
- key_weight_grad: float32 [2, 1280, 1280], P(None, 'shard')
- value_weight_grad: float32 [2, 1280, 1280], P(None, 'shard')
- value_bias_grad: float32 [2, 1280], P(None, 'shard')
- out_weight_grad: float32 [2, 1280, 1280], P(None, 'shard')
- out_bias_grad: float32 [2, 1280], P(None, 'shard')
- mlp_gain_grad: float32 [2, 1280], P(None, 'shard')
- mlp_shift_grad: float32 [2, 1280], P(None, 'shard')
- up_weight_grad: float32 [2, 1280, 5120], P(None, 'shard')
- up_bias_grad: float32 [2, 5120], P(None, 'shard')
- down_weight_grad: float32 [2, 5120, 1280], P(None, 'shard')
- down_bias_grad: float32 [2, 1280], P(None, 'shard')
Inputs may be any that keep to these rules, and one draw needn't show every extreme that they name: `lengths`: of the 2 clips on one index of rep, one (which, drawn from the seed) has all 1024 tokens valid.
All inputs are finite; a program needn't handle non-finite values.
Results may differ from a plain program's by a relative error of at most 0.02.
Values may be sent and summed in bfloat16 or wider, within the bound.
A program may use at most 576 MiB of HBM per device.

v0:
```python
import functools
import math

import jax
import jax.numpy as jnp
from jax import lax
from jax.experimental import pallas as pl
from jax.experimental.pallas import tpu as pltpu
from jax.sharding import PartitionSpec as P

H = 16
EPSILON = 1e-05
NEGATIVE = -1e30
BF16 = jnp.bfloat16
F32 = jnp.float32
BOTH = ("rep", "shard")


def norm_affine(values, norm_gain, norm_shift):
    center = values - jnp.mean(values, axis=-1, keepdims=True)
    spread = jnp.mean(center * center, axis=-1, keepdims=True)
    return center * lax.rsqrt(spread + EPSILON) * norm_gain + norm_shift


def gelu_exact(values):
    return jax.nn.gelu(values, approximate=False)


def project(left_operand, right_operand):
    return jnp.einsum(
        "csa,ab->csb", left_operand, right_operand, preferred_element_type=jnp.float32
    )


def project_back(left_operand, right_operand):
    return jnp.einsum(
        "csb,ab->csa", left_operand, right_operand, preferred_element_type=jnp.float32
    )


def weight_grad(left_operand, right_operand):
    return jnp.einsum(
        "csa,csb->ab", left_operand, right_operand, preferred_element_type=jnp.float32
    )


def column_sum(values):
    return jnp.sum(values.astype(jnp.float32), axis=(0, 1))


def layer_slice(params, layer_index):
    return tuple((weight_array[layer_index] for weight_array in params))


def fetch_forward(local_params):
    return (
        lax.all_gather(local_params[0], "shard", axis=0, tiled=True),
        lax.all_gather(local_params[1], "shard", axis=0, tiled=True),
        lax.all_gather(local_params[2], "shard", axis=0, tiled=True),
        lax.all_gather(local_params[3], "shard", axis=0, tiled=True),
        lax.all_gather(local_params[4], "shard", axis=0, tiled=True),
        lax.all_gather(local_params[5], "shard", axis=0, tiled=True),
        lax.all_gather(local_params[6], "shard", axis=0, tiled=True),
        lax.all_gather(local_params[7], "shard", axis=0, tiled=True),
        lax.all_gather(local_params[8], "shard", axis=0, tiled=True),
        lax.all_gather(local_params[9], "shard", axis=0, tiled=True),
        lax.all_gather(local_params[10], "shard", axis=0, tiled=True),
        lax.all_gather(local_params[11], "shard", axis=0, tiled=True),
        lax.all_gather(local_params[12], "shard", axis=0, tiled=True),
        lax.all_gather(local_params[13], "shard", axis=0, tiled=True),
        lax.all_gather(local_params[14], "shard", axis=0, tiled=True),
    )


def fetch_again(local_params):
    return (
        lax.all_gather(local_params[0], "shard", axis=0, tiled=True),
        lax.all_gather(local_params[1], "shard", axis=0, tiled=True),
        lax.all_gather(local_params[2], "shard", axis=0, tiled=True),
        lax.all_gather(local_params[3], "shard", axis=0, tiled=True),
        lax.all_gather(local_params[4], "shard", axis=0, tiled=True),
        lax.all_gather(local_params[5], "shard", axis=0, tiled=True),
        lax.all_gather(local_params[6], "shard", axis=0, tiled=True),
        lax.all_gather(local_params[7], "shard", axis=0, tiled=True),
        lax.all_gather(local_params[8], "shard", axis=0, tiled=True),
        lax.all_gather(local_params[9], "shard", axis=0, tiled=True),
        lax.all_gather(local_params[10], "shard", axis=0, tiled=True),
        lax.all_gather(local_params[11], "shard", axis=0, tiled=True),
        lax.all_gather(local_params[12], "shard", axis=0, tiled=True),
        lax.all_gather(local_params[13], "shard", axis=0, tiled=True),
        lax.all_gather(local_params[14], "shard", axis=0, tiled=True),
    )


def forward_layer(hidden_state, weights, lengths):
    (
        attn_gain,
        attn_shift,
        query_weight,
        query_bias,
        key_weight,
        value_weight,
        value_bias,
        out_weight,
        out_bias,
        mlp_gain,
        mlp_shift,
        up_weight,
        up_bias,
        down_weight,
        down_bias,
    ) = weights
    clip_count, row_count, model_width = hidden_state.shape
    head_size = model_width // H
    query_scale = float(head_size) ** (-0.5)
    normed = norm_affine(
        hidden_state, attn_gain.astype(jnp.float32), attn_shift.astype(jnp.float32)
    ).astype(jnp.bfloat16)
    query_low = (
        (project(normed, query_weight) + query_bias.astype(jnp.float32)) * query_scale
    ).astype(jnp.bfloat16)
    key_low = project(normed, key_weight).astype(jnp.bfloat16)
    value_low = (project(normed, value_weight) + value_bias.astype(jnp.float32)).astype(
        jnp.bfloat16
    )
    key_all, value_all = (
        lax.all_gather(key_low, "shard", axis=1, tiled=True),
        lax.all_gather(value_low, "shard", axis=1, tiled=True),
    )
    length_all = key_all.shape[1]
    valid_keys = jnp.arange(length_all, dtype=jnp.int32)[None, :] < lengths[:, None]
    query_heads = query_low.reshape(clip_count, row_count, H, head_size)
    key_heads = key_all.reshape(clip_count, length_all, H, head_size)
    value_heads = value_all.reshape(clip_count, length_all, H, head_size)
    scores = jnp.einsum(
        "cqhd,ckhd->chqk", query_heads, key_heads, preferred_element_type=jnp.float32
    )
    scores = jnp.where(valid_keys[:, None, None, :], scores, NEGATIVE)
    attention = jax.nn.softmax(scores, axis=-1)
    attention_low = attention.astype(jnp.bfloat16)
    context = jnp.einsum(
        "chqk,ckhd->cqhd", attention_low, value_heads, preferred_element_type=jnp.float32
    )
    context_low = context.reshape(clip_count, row_count, model_width).astype(jnp.bfloat16)
    middle = hidden_state + project(context_low, out_weight) + out_bias.astype(jnp.float32)
    hidden_in = norm_affine(
        middle, mlp_gain.astype(jnp.float32), mlp_shift.astype(jnp.float32)
    ).astype(jnp.bfloat16)
    pre_gelu = project(hidden_in, up_weight) + up_bias.astype(jnp.float32)
    active_low = gelu_exact(pre_gelu).astype(jnp.bfloat16)
    result = middle + project(active_low, down_weight) + down_bias.astype(jnp.float32)
    kept_values = (
        normed,
        query_heads,
        key_heads,
        value_heads,
        attention,
        attention_low,
        context_low,
        middle,
        hidden_in,
        pre_gelu,
        active_low,
    )
    return (result, kept_values)


def backward_layer(hidden_state, grad_after, weights, lengths):
    (
        attn_gain,
        attn_shift,
        query_weight,
        query_bias,
        key_weight,
        value_weight,
        value_bias,
        out_weight,
        out_bias,
        mlp_gain,
        mlp_shift,
        up_weight,
        up_bias,
        down_weight,
        down_bias,
    ) = weights
    unused, kept_values = forward_layer(hidden_state, weights, lengths)
    (
        normed,
        query_heads,
        key_heads,
        value_heads,
        attention,
        attention_low,
        context_low,
        middle,
        hidden_in,
        pre_gelu,
        active_low,
    ) = kept_values
    clip_count, row_count, model_width = hidden_state.shape
    length_all = key_heads.shape[1]
    head_size = model_width // H
    query_scale = float(head_size) ** (-0.5)
    grad_low = grad_after.astype(jnp.bfloat16)
    grad_active = project_back(grad_low, down_weight)
    unused, gelu_pull = jax.vjp(gelu_exact, pre_gelu)
    grad_pre = gelu_pull(grad_active)[0].astype(jnp.bfloat16)
    grad_hidden = project_back(grad_pre, up_weight)
    unused, mlp_pull = jax.vjp(
        norm_affine, middle, mlp_gain.astype(jnp.float32), mlp_shift.astype(jnp.float32)
    )
    grad_middle_norm, grad_mlp_gain, grad_mlp_shift = mlp_pull(grad_hidden)
    grad_middle = grad_after + grad_middle_norm
    middle_low = grad_middle.astype(jnp.bfloat16)
    grad_context = project_back(middle_low, out_weight).astype(jnp.bfloat16)
    grad_context = grad_context.reshape(clip_count, row_count, H, head_size)
    grad_attention = jnp.einsum(
        "cqhd,ckhd->chqk", grad_context, value_heads, preferred_element_type=jnp.float32
    )
    value_part = jnp.einsum(
        "chqk,cqhd->ckhd", attention_low, grad_context, preferred_element_type=jnp.float32
    )
    grad_scores = attention * (
        grad_attention - jnp.sum(attention * grad_attention, axis=-1, keepdims=True)
    )
    scores_low = grad_scores.astype(jnp.bfloat16)
    grad_query = jnp.einsum(
        "chqk,ckhd->cqhd", scores_low, key_heads, preferred_element_type=jnp.float32
    )
    grad_query = grad_query.reshape(clip_count, row_count, model_width).astype(jnp.bfloat16)
    key_part = jnp.einsum(
        "chqk,cqhd->ckhd", scores_low, query_heads, preferred_element_type=jnp.float32
    )
    key_summed, value_summed = (
        lax.psum_scatter(
            key_part.reshape(clip_count, length_all, model_width).astype(jnp.bfloat16),
            "shard",
            scatter_dimension=1,
            tiled=True,
        ).astype(jnp.float32),
        lax.psum_scatter(
            value_part.reshape(clip_count, length_all, model_width).astype(jnp.bfloat16),
            "shard",
            scatter_dimension=1,
            tiled=True,
        ).astype(jnp.float32),
    )
    key_grad_low = key_summed.astype(jnp.bfloat16)
    value_grad_low = value_summed.astype(jnp.bfloat16)
    grad_normed = (
        project_back(grad_query, query_weight) * query_scale
        + project_back(key_grad_low, key_weight)
        + project_back(value_grad_low, value_weight)
    )
    unused, attn_pull = jax.vjp(
        norm_affine, hidden_state, attn_gain.astype(jnp.float32), attn_shift.astype(jnp.float32)
    )
    grad_input_norm, grad_attn_gain, grad_attn_shift = attn_pull(grad_normed)
    grad_before = grad_middle + grad_input_norm
    grad_down = weight_grad(active_low, grad_low)
    grad_down_bias = column_sum(grad_low)
    grad_up = weight_grad(hidden_in, grad_pre)
    grad_up_bias = column_sum(grad_pre)
    grad_out_weight = weight_grad(context_low, middle_low)
    grad_out_bias = column_sum(middle_low)
    grad_query_weight = weight_grad(normed, grad_query) * query_scale
    grad_query_bias = column_sum(grad_query) * query_scale
    grad_key_weight = weight_grad(normed, key_grad_low)
    grad_value_weight = weight_grad(normed, value_grad_low)
    grad_value_bias = column_sum(value_grad_low)
    owned_grads = (
        lax.psum_scatter(
            grad_attn_gain.astype(jnp.bfloat16), "shard", scatter_dimension=0, tiled=True
        ).astype(jnp.float32),
        lax.psum_scatter(
            grad_attn_shift.astype(jnp.bfloat16), "shard", scatter_dimension=0, tiled=True
        ).astype(jnp.float32),
        lax.psum_scatter(
            grad_query_weight.astype(jnp.bfloat16), "shard", scatter_dimension=0, tiled=True
        ).astype(jnp.float32),
        lax.psum_scatter(
            grad_query_bias.astype(jnp.bfloat16), "shard", scatter_dimension=0, tiled=True
        ).astype(jnp.float32),
        lax.psum_scatter(
            grad_key_weight.astype(jnp.bfloat16), "shard", scatter_dimension=0, tiled=True
        ).astype(jnp.float32),
        lax.psum_scatter(
            grad_value_weight.astype(jnp.bfloat16), "shard", scatter_dimension=0, tiled=True
        ).astype(jnp.float32),
        lax.psum_scatter(
            grad_value_bias.astype(jnp.bfloat16), "shard", scatter_dimension=0, tiled=True
        ).astype(jnp.float32),
        lax.psum_scatter(
            grad_out_weight.astype(jnp.bfloat16), "shard", scatter_dimension=0, tiled=True
        ).astype(jnp.float32),
        lax.psum_scatter(
            grad_out_bias.astype(jnp.bfloat16), "shard", scatter_dimension=0, tiled=True
        ).astype(jnp.float32),
        lax.psum_scatter(
            grad_mlp_gain.astype(jnp.bfloat16), "shard", scatter_dimension=0, tiled=True
        ).astype(jnp.float32),
        lax.psum_scatter(
            grad_mlp_shift.astype(jnp.bfloat16), "shard", scatter_dimension=0, tiled=True
        ).astype(jnp.float32),
        lax.psum_scatter(
            grad_up.astype(jnp.bfloat16), "shard", scatter_dimension=0, tiled=True
        ).astype(jnp.float32),
        lax.psum_scatter(
            grad_up_bias.astype(jnp.bfloat16), "shard", scatter_dimension=0, tiled=True
        ).astype(jnp.float32),
        lax.psum_scatter(
            grad_down.astype(jnp.bfloat16), "shard", scatter_dimension=0, tiled=True
        ).astype(jnp.float32),
        lax.psum_scatter(
            grad_down_bias.astype(jnp.bfloat16), "shard", scatter_dimension=0, tiled=True
        ).astype(jnp.float32),
    )
    return (grad_before, owned_grads)


def replica_layer(owned_grads):
    return (
        lax.psum(owned_grads[0].astype(jnp.bfloat16), "rep").astype(jnp.float32),
        lax.psum(owned_grads[1].astype(jnp.bfloat16), "rep").astype(jnp.float32),
        lax.psum(owned_grads[2].astype(jnp.bfloat16), "rep").astype(jnp.float32),
        lax.psum(owned_grads[3].astype(jnp.bfloat16), "rep").astype(jnp.float32),
        lax.psum(owned_grads[4].astype(jnp.bfloat16), "rep").astype(jnp.float32),
        lax.psum(owned_grads[5].astype(jnp.bfloat16), "rep").astype(jnp.float32),
        lax.psum(owned_grads[6].astype(jnp.bfloat16), "rep").astype(jnp.float32),
        lax.psum(owned_grads[7].astype(jnp.bfloat16), "rep").astype(jnp.float32),
        lax.psum(owned_grads[8].astype(jnp.bfloat16), "rep").astype(jnp.float32),
        lax.psum(owned_grads[9].astype(jnp.bfloat16), "rep").astype(jnp.float32),
        lax.psum(owned_grads[10].astype(jnp.bfloat16), "rep").astype(jnp.float32),
        lax.psum(owned_grads[11].astype(jnp.bfloat16), "rep").astype(jnp.float32),
        lax.psum(owned_grads[12].astype(jnp.bfloat16), "rep").astype(jnp.float32),
        lax.psum(owned_grads[13].astype(jnp.bfloat16), "rep").astype(jnp.float32),
        lax.psum(owned_grads[14].astype(jnp.bfloat16), "rep").astype(jnp.float32),
    )


def general_shards(
    inputs,
    lengths,
    cotangent,
    attn_gain,
    attn_shift,
    query_weight,
    query_bias,
    key_weight,
    value_weight,
    value_bias,
    out_weight,
    out_bias,
    mlp_gain,
    mlp_shift,
    up_weight,
    up_bias,
    down_weight,
    down_bias,
):
    params = (
        attn_gain,
        attn_shift,
        query_weight,
        query_bias,
        key_weight,
        value_weight,
        value_bias,
        out_weight,
        out_bias,
        mlp_gain,
        mlp_shift,
        up_weight,
        up_bias,
        down_weight,
        down_bias,
    )
    layers = attn_gain.shape[0]
    hidden_state = inputs.astype(jnp.float32)
    kept_inputs = []
    kept_weights = []
    for layer_index in range(layers):
        gathered = fetch_forward(layer_slice(params, layer_index))
        kept_inputs.append(hidden_state)
        kept_weights.append(gathered)
        hidden_state, unused = forward_layer(hidden_state, gathered, lengths)
    output = hidden_state.astype(jnp.bfloat16)
    row_count = inputs.shape[1]
    first_row = lax.axis_index("shard") * row_count
    positions = first_row + jnp.arange(row_count, dtype=jnp.int32)
    row_mask = (positions[None, :] < lengths[:, None]).astype(jnp.float32)
    grad_state = cotangent.astype(jnp.float32) * row_mask[:, :, None]
    owned_list = [None] * layers
    for layer_index in reversed(range(layers)):
        gathered = fetch_again(layer_slice(params, layer_index))
        grad_state, owned_grads = backward_layer(
            kept_inputs[layer_index], grad_state, gathered, lengths
        )
        owned_grads = replica_layer(owned_grads)
        owned_list[layer_index] = owned_grads
    stacked = tuple(
        (
            jnp.stack([owned_list[layer_index][member] for layer_index in range(layers)])
            for member in range(15)
        )
    )
    return (
        output,
        grad_state,
        stacked[0],
        stacked[1],
        stacked[2],
        stacked[3],
        stacked[4],
        stacked[5],
        stacked[6],
        stacked[7],
        stacked[8],
        stacked[9],
        stacked[10],
        stacked[11],
        stacked[12],
        stacked[13],
        stacked[14],
    )


def device_index(a, b, core, z):
    return ((a * 2 + b) * 2 + core) * 4 + z


def make_pairs(target):
    return [
        (device_index(a, b, core, z), device_index(*target(a, b, core, z)))
        for a in range(2)
        for b in range(2)
        for core in range(2)
        for z in range(4)
    ]


PAIRS = {
    "a": make_pairs(lambda a, b, c, z: (1 - a, b, c, z)),
    "b": make_pairs(lambda a, b, c, z: (a, 1 - b, c, z)),
    "ab": make_pairs(lambda a, b, c, z: (1 - a, 1 - b, c, z)),
    "core": make_pairs(lambda a, b, c, z: (a, b, 1 - c, z)),
    "z1": make_pairs(lambda a, b, c, z: (a, b, c, (z + 1) % 4)),
    "z2": make_pairs(lambda a, b, c, z: (a, b, c, (z + 2) % 4)),
    "z3": make_pairs(lambda a, b, c, z: (a, b, c, (z + 3) % 4)),
}
for step in range(2):
    PAIRS["in%d" % step] = make_pairs(
        lambda a, b, c, z, step=step: (a, b, z // 2, 2 * c + (z + step) % 2)
    )
    PAIRS["out%d" % step] = [(target, source) for source, target in PAIRS["in%d" % step]]


def send(values, way):
    return lax.ppermute(values, BOTH, PAIRS[way])


def pick(values, index, axis=0):
    return lax.dynamic_index_in_dim(values, index, axis, keepdims=False)


def place():
    rep = lax.axis_index("rep")
    return rep // 4, (rep // 2) % 2, rep % 2, lax.axis_index("shard")


def after(values, *others):
    return lax.optimization_barrier((values,) + others)[0]


MESH = pl.DeviceIdType.MESH

def device(a, b, core, z):
    return ((a * 2 + b) * 2 + core, z)


class Net:
    def __init__(self, sent, arrived):
        self.sent, self.arrived = sent, arrived
        self.copies, self.count = [], 0
    def push(self, source, target_ref, target, sent=None):
        copy = pltpu.make_async_remote_copy(
            src_ref=source, dst_ref=target_ref, send_sem=self.sent if sent is None else sent,
            recv_sem=self.arrived.at[self.count], device_id=target, device_id_type=MESH)
        copy.start()
        self.count += 1
        if sent is None:
            self.copies.append(copy)
        return copy

    def drain(self):
        for copy in self.copies:
            copy.wait_send()

def greet(targets):
    barrier = pltpu.get_barrier_semaphore()
    for target in targets:
        pl.semaphore_signal(barrier, inc=1, device_id=target, device_id_type=MESH)
    pl.semaphore_wait(barrier, len(targets))

def gather_regions(index, zs, chip, core):
    part = chip * 2 + core
    def rows(base, size):
        return pl.ds(pl.multiple_of(base, 8), size)
    if index < 2:
        return 0, (pl.ds(2 * index, 2), rows(zs * 320 + part * 40, 40), slice(None))
    if index < 4:
        return 1, (rows(zs * 320 + part * 40, 40), pl.ds((index - 2) * 2560, 2560))
    return 2, (rows(zs * 1280 + part * 160 + (index - 4) * 80, 80), slice(None))


NN = (((1,), (0,)), ((), ()))
TN = (((0,), (0,)), ((), ()))
NT = (((1,), (1,)), ((), ()))
TOKENS = 512
ROOT_HALF = math.sqrt(0.5)
ROOT_TWO_PI = math.sqrt(2.0 * math.pi)

def dot(left, right, numbers=NN):
    return lax.dot_general(left, right, numbers, preferred_element_type=F32)


def tile(i, size):
    return pl.ds(pl.multiple_of(i * size, size), size)


def stream(count, copy, body):
    copy(0, 0).start()

    @pl.loop(0, count)
    def _(i):
        slot = i % 2

        @pl.when(i + 1 < count)
        def _():
            copy(i + 1, 1 - slot).start()

        copy(i, slot).wait()
        body(i, slot)


def transpose_into(target, source, rows):
    @pl.loop(0, rows // 128)
    def _(i):
        target[tile(i, 128), :] = source[:, tile(i, 128)].T


def gather_program(net, layers, shards, outs, copies, local):
    a, b, core, z = place()
    behind = [lax.rem(z + 4 - s, 4) for s in range(4)]
    to_z = [device(a, b, core, lax.rem(z + s, 4)) for s in range(4)]
    to_a, to_b, to_core = device(1 - a, b, core, z), device(a, 1 - b, core, z), device(a, b, 1 - core, z)
    count = 6 * layers
    twin = [[] for _ in range(count)]

    def refs_at(index, zs, pa, pb, whose):
        which, at = gather_regions(index % 6, zs, pa * 2 + pb, core)
        return whose[which].at[index // 6].at[at]

    def start(index):
        return [net.push(refs_at(index, 0, a, b, shards), refs_at(index, z, a, b, outs), to_z[s]) for s in (1, 2, 3)]

    def on(index, s, pa, pb, target):
        ref = refs_at(index, behind[s], pa, pb, outs)
        copy = net.push(ref, ref, target)
        if target is to_core:
            twin[index].append(copy)
        return copy

    def own_copies(step):
        layer, which = step // 3, step % 3
        shard, out = shards[which].at[layer], outs[which].at[layer]
        ins, back = [], []
        for i in range(4):
            if which == 0:
                source, target = shard.at[i], out.at[i, pl.ds(pl.multiple_of(z * 320, 8), 320), :]
            elif which == 1:
                source = shard.at[:, pl.ds(i * 1280, 1280)]
                target = out.at[pl.ds(pl.multiple_of(z * 320, 8), 320), pl.ds(i * 1280, 1280)]
            else:
                source = shard.at[pl.ds(i * 320, 320), :]
                target = out.at[pl.ds(pl.multiple_of(z * 1280 + i * 320, 8), 320), :]
            ins.append(pltpu.make_async_copy(source, copies.at[i], local))
            back.append(pltpu.make_async_copy(copies.at[i], target, local))
        for copy in ins:
            copy.start()
        for copy in ins:
            copy.wait()
        for copy in back:
            copy.start()
        for copy in back:
            copy.wait()

    zed, mid, diag = {}, {}, {}
    zed[0] = start(0)
    zed[1] = start(1)
    own_copies(0)
    yield twin
    for t in range(count + 2):
        if t < count:
            mid[t] = {}
            for s in (1, 2, 3):
                zed[t][s - 1].wait_recv()
                mid[t][s] = (on(t, s, a, b, to_b), on(t, s, a, b, to_a))
                on(t, s, a, b, to_core)
            if t + 2 < count:
                zed[t + 2] = start(t + 2)
        if 0 <= t - 1 < count:
            k = t - 1
            diag[k] = {}
            for s in (1, 2, 3):
                via_b, via_a = mid[k][s]
                via_b.wait_recv()
                on(k, s, a, 1 - b, to_core)
                if (s + k) % 2 == 0:
                    diag[k][s] = on(k, s, a, 1 - b, to_a)
                via_a.wait_recv()
                on(k, s, 1 - a, b, to_core)
                if (s + k) % 2 == 1:
                    diag[k][s] = on(k, s, 1 - a, b, to_b)
        if 0 <= t - 2 < count:
            k = t - 2
            for s in (1, 2, 3):
                diag[k][s].wait_recv()
                on(k, s, 1 - a, 1 - b, to_core)
        if t + 1 < 3 * layers:
            own_copies(t + 1)
        yield twin


def normalize_rows(source, target, gain, shift, rows=64):
    @pl.loop(0, TOKENS // rows)
    def _(i):
        values = source[tile(i, rows), :]
        center = values - jnp.mean(values, axis=-1, keepdims=True)
        scale = lax.rsqrt(jnp.mean(center * center, axis=-1, keepdims=True) + EPSILON)
        target[tile(i, rows), :] = (center * scale * gain + shift).astype(BF16)


def attend_heads(first, last, query, key, value, far, masks, context, lse):
    @pl.loop(first, last)
    def _(h):
        at = pl.ds(pl.multiple_of(h * 80, 16), 80)
        q = query[at, :]
        s0 = dot(key[at, :], q, TN) + masks[0]
        s1 = dot(far[0, at, :], q, TN) + masks[1]
        top = jnp.maximum(jnp.max(s0, axis=0, keepdims=True), jnp.max(s1, axis=0, keepdims=True))
        e0, e1 = jnp.exp(s0 - top), jnp.exp(s1 - top)
        total = jnp.sum(e0, axis=0, keepdims=True) + jnp.sum(e1, axis=0, keepdims=True)
        out = dot(value[at, :], e0.astype(BF16)) + dot(far[1, at, :], e1.astype(BF16))
        context[at, :] = (out / total).astype(BF16)
        lse[h] = top + jnp.log(total)


def forward_kernel(layers, *refs):
    (tokens, attn, up, down, vectors, masks,
     attn_full, up_full, down_full, keep_normed, keep_qkv, keep_far, keep_lse, keep_context, keep_middle,
     keep_hidden, keep_slope, keep_active, states,
     state, middle, normed, normed_t, hidden_t, qkv, far, context_t, context, active, active_t, slope, lse,
     small_w, up_w, down_w, copies, product,
     local, wsem, saved, swapped, sent, arrived) = refs
    a, b, core, z = place()
    to_core = device(a, b, 1 - core, z)
    greet([device(a, b, core, lax.rem(z + s, 4)) for s in (1, 2, 3)]
          + [device(1 - a, b, core, z), device(a, 1 - b, core, z), to_core])
    net = Net(sent, arrived)
    load = pltpu.make_async_copy(tokens, state, local)
    load.start()
    load.wait()
    ticks = gather_program(net, layers, (attn, up, down), (attn_full, up_full, down_full), copies, local)
    twin = next(ticks)
    clock = [-1]

    def pump(until):
        while clock[0] < until:
            next(ticks)
            clock[0] += 1

    def ready(*chunks):
        pump(max(chunks) + 2)
        for chunk in chunks:
            for copy in twin[chunk]:
                copy.wait_recv()

    saves = []

    def save(source, target):
        copy = pltpu.make_async_copy(source, target, saved)
        copy.start()
        saves.append(copy)

    scale = float(80) ** (-0.5)
    for layer in range(layers):
        base = 6 * layer
        vec = vectors.at[layer]

        def row(i):
            return vec[i : i + 1, :]

        weights = attn_full.at[layer]
        save(state, states.at[layer])
        normalize_rows(state, normed, row(0), row(1))
        transpose_into(normed_t, normed, 1280)
        save(normed_t, keep_normed.at[layer])
        ready(base, base + 1)

        def project(which, bias, factor, target):
            def copy(i, slot):
                return pltpu.make_async_copy(weights.at[which, :, tile(i, 256)], small_w.at[slot], wsem.at[slot])

            def body(i, slot):
                out = dot(normed[...], small_w[slot])
                if bias is not None:
                    out = out + vec[bias : bias + 1, tile(i, 256)]
                if factor != 1.0:
                    out = out * factor
                target[tile(i, 256), :] = out.astype(BF16).T

            stream(5, copy, body)

        project(1, None, 1.0, qkv.at[1])
        project(2, 3, 1.0, qkv.at[2])
        swap = net.push(qkv.at[pl.ds(1, 2)], far.at[layer], to_core, swapped)
        project(0, 2, scale, qkv.at[0])
        pump(base + 4)
        swap.wait()
        for part in range(4):
            if part == 2:
                pump(base + 5)
            attend_heads(4 * part, 4 * part + 4, qkv.at[0], qkv.at[1], qkv.at[2], far.at[layer], masks, context_t, lse)
        save(qkv, keep_qkv.at[layer])
        save(far.at[layer], keep_far.at[layer])
        save(lse, keep_lse.at[layer])
        save(context_t, keep_context.at[layer])

        @pl.loop(0, 10)
        def _(i):
            context[:, tile(i, 128)] = context_t[tile(i, 128), :].T

        def copy_out(i, slot):
            return pltpu.make_async_copy(weights.at[3, :, tile(i, 256)], small_w.at[slot], wsem.at[slot])

        def body_out(i, slot):
            at = tile(i, 256)
            middle[:, at] = state[:, at] + dot(context[...], small_w[slot]) + vec[4:5, at]

        stream(5, copy_out, body_out)
        save(middle, keep_middle.at[layer])
        normalize_rows(middle, normed, row(5), row(6))
        transpose_into(hidden_t, normed, 1280)
        save(hidden_t, keep_hidden.at[layer])
        pump(base + 6)
        ready(base + 2, base + 3)

        def copy_up(i, slot):
            return pltpu.make_async_copy(up_full.at[layer, :, tile(i, 512)], up_w.at[slot], wsem.at[slot])

        def body_up(i, slot):
            at = tile(i, 512)
            product[...] = dot(normed[...], up_w[slot])
            bias = vec[pl.ds(8 + i, 1), :512]

            @pl.loop(0, 16)
            def _(j):
                u = product[tile(j, 32), :] + bias
                half = 0.5 * (1.0 + lax.erf(u * ROOT_HALF))
                active[tile(j, 32), at] = (u * half).astype(BF16)
                slope[tile(j, 32), at] = (half + u * jnp.exp(-0.5 * u * u) * (1.0 / ROOT_TWO_PI)).astype(BF16)

            active_t[at, :] = active[:, at].T

        stream(10, copy_up, body_up)
        save(slope, keep_slope.at[layer])
        save(active_t, keep_active.at[layer])
        ready(base + 4, base + 5)

        def copy_down(i, slot):
            return pltpu.make_async_copy(down_full.at[layer, :, tile(i, 256)], down_w.at[slot], wsem.at[slot])

        for copy in saves:
            copy.wait()
        saves.clear()

        def body_down(i, slot):
            at = tile(i, 256)
            state[:, at] = middle[:, at] + dot(active[...], down_w[slot]) + vec[7:8, at]

        stream(5, copy_down, body_down)
    save(state, states.at[layers])
    for copy in saves:
        copy.wait()
    net.drain()


def forward_all(tokens, attn, up, down, vectors, masks):
    any_ = pl.BlockSpec(memory_space=pl.ANY)
    vmem = pl.BlockSpec(memory_space=pltpu.VMEM)
    layers = up.shape[0]
    t = TOKENS

    def hbm(shape, dtype=BF16):
        return jax.ShapeDtypeStruct((layers,) + shape, dtype)

    out_shape = (
        hbm((4, 1280, 1280)), hbm((1280, 5120)), hbm((5120, 1280)),
        hbm((1280, t)), hbm((3, 1280, t)), hbm((2, 1280, t)), hbm((H, 1, t), F32), hbm((1280, t)), hbm((t, 1280), F32),
        hbm((1280, t)), hbm((t, 5120)), hbm((5120, t)), jax.ShapeDtypeStruct((layers + 1, t, 1280), F32),
    )
    v = pltpu.VMEM
    return pl.pallas_call(
        functools.partial(forward_kernel, layers),
        out_shape=out_shape,
        in_specs=[any_] * 4 + [vmem] * 2,
        out_specs=(any_,) * len(out_shape),
        scratch_shapes=[
            v((t, 1280), F32), v((t, 1280), F32), v((t, 1280), BF16), v((1280, t), BF16), v((1280, t), BF16),
            v((3, 1280, t), BF16), v((layers, 2, 1280, t), BF16), v((1280, t), BF16), v((t, 1280), BF16),
            v((t, 5120), BF16), v((5120, t), BF16), v((t, 5120), BF16), v((H, 1, t), F32),
            v((2, 1280, 256), BF16), v((2, 1280, 512), BF16), v((2, 5120, 256), BF16), v((4, 320, 1280), BF16),
            v((t, 512), F32),
            pltpu.SemaphoreType.DMA, pltpu.SemaphoreType.DMA((2,)), pltpu.SemaphoreType.DMA,
            pltpu.SemaphoreType.DMA, pltpu.SemaphoreType.DMA, pltpu.SemaphoreType.DMA((6 * layers * 24 + layers,)),
        ],
        compiler_params=pltpu.CompilerParams(collective_id=1, has_side_effects=True, vmem_limit_bytes=63 << 20),
        name="forward_all",
    )(tokens, attn, up, down, vectors, masks)


def add(*parts):
    total = parts[0].astype(F32)
    for part in parts[1:]:
        total = total + part.astype(F32)
    return total.astype(BF16)


ITEMS_A_LAYER = 12
RING, XRING = 8, 4


def streams(count, copies, body):
    for copy in copies(0, 0):
        copy.start()

    @pl.loop(0, count)
    def _(i):
        slot = i % 2

        @pl.when(i + 1 < count)
        def _():
            for copy in copies(i + 1, 1 - slot):
                copy.start()

        for copy in copies(i, slot):
            copy.wait()
        body(i, slot)


def add_blocks(blocks, target, parts):
    @pl.loop(0, blocks * 5)
    def _(i):
        block = i // 5
        at = pl.ds(pl.multiple_of((i % 5) * 16, 16), 16)
        refs = [part(block) for part in parts]
        sums = refs[0][at, :].astype(F32)
        for ref in refs[1:]:
            sums = sums + ref[at, :].astype(F32)
        target(block)[at, :] = sums.astype(BF16)


def backward_kernel(layers, *refs):
    (cotangent, attn_full, up_full, down_full, normed_t, qkv, far, lse_all, context_t, middles, hidden_t, slopes,
     active_t, states, vectors, masks,
     grad_out, down_out, up_out, out_out, qkv_out, sums,
     active_far, hidden_far, context_far, normed_far, grad_f_far, grad_pre_far, grad_o_far, grad_far, grad_kv_far,
     g, low, gp, gs, gh, rows_in, big, dfar, heads_in, far_in, lse, wide_w, slope_in, left_in,
     xs, got1s, got2s, got3s, finals,
     local, lsem, swapped, item_sent, item_local, sent, arrived) = refs
    a, b, core, z = place()
    to_z = [device(a, b, core, lax.rem(z + s, 4)) for s in range(4)]
    to_a, to_b, to_core = device(1 - a, b, core, z), device(a, 1 - b, core, z), device(a, b, 1 - core, z)
    greet(to_z[1:] + [to_a, to_b, to_core])
    net = Net(sent, arrived)
    scale = float(80) ** (-0.5)
    side = {"a": (a, to_a), "b": (b, to_b)}

    def program(number, order, spot):
        slot = number % RING
        x, got1, got2, got3, final = (
            xs.at[number % XRING], got1s.at[slot], got2s.at[slot], got3s.at[slot], finals.at[slot])
        target = side[order[0]][1]
        other, other_target = side["b" if order[0] == "a" else "a"]

        def push(source, target_ref, target, stage):
            return net.push(source, target_ref, target, item_sent.at[slot, stage])

        first = push(x.at[1], got1, target, 0)
        yield
        first.wait()
        add_blocks(8, lambda i: got1.at[i // 2, i % 2],
                   [lambda i: got1.at[i // 2, i % 2], lambda i: x.at[0, i // 2, i % 2]])
        if order[1] == "z":
            nexts = [push(got1.at[lax.rem(z + s, 4)], got2.at[pl.ds(2 * s - 2, 2)], to_z[s], 1) for s in (1, 2, 3)]
        else:
            nexts = [push(got1.at[:, 1 - other], got2.at[pl.ds(0, 4)], other_target, 1)]
        yield
        for copy in nexts:
            copy.wait()
        if order[1] == "z":
            add_blocks(2, lambda i: got1.at[z, i],
                       [lambda i: got1.at[z, i]] + [lambda i, s=s: got2.at[2 * s + i] for s in range(3)])
            nexts = [push(got1.at[z, 1 - other], got3.at[0], other_target, 2)]
        else:
            add_blocks(4, lambda i: got2.at[i], [lambda i: got2.at[i], lambda i: got1.at[i, other]])
            nexts = [push(got2.at[lax.rem(z + s, 4)], got3.at[s - 1], to_z[s], 2) for s in (1, 2, 3)]
        yield
        for copy in nexts:
            copy.wait()
        if order[1] == "z":
            add_blocks(1, lambda i: final, [lambda i: got1.at[z, other], lambda i: got3.at[0]])
        else:
            add_blocks(1, lambda i: final, [lambda i: got2.at[z]] + [lambda i, s=s: got3.at[s] for s in range(3)])
        mine = pltpu.make_async_copy(final, spot(core, a, b), item_local.at[slot])
        mine.start()
        via = [push(final, spot(core, a, b), target, 3) for target in (to_a, to_b, to_core)]
        yield
        mine.wait()
        for copy in via:
            copy.wait()

        def on(pa, pb, target):
            return net.push(spot(core, pa, pb), spot(core, pa, pb), target)

        diag = on(1 - a, b, to_b) if number % 2 == 0 else on(a, 1 - b, to_a)
        twin = [on(1 - a, b, to_core), on(a, 1 - b, to_core)]
        yield
        diag.wait_recv()
        twin.append(on(1 - a, 1 - b, to_core))
        yield
        for copy in twin:
            copy.wait_recv()
        yield

    programs, stage, age = [], [], []

    def advance(number):
        next(programs[number])
        stage[number] += 1

    def round_(lead=1):
        for number in range(len(programs)):
            age[number] += 1
            if stage[number] < 7 and (stage[number] > 1 or age[number] >= lead):
                advance(number)

    def room(extra):
        while any(stage[i] < 2 for i in range(max(0, len(programs) + extra - XRING))):
            round_()
        while any(stage[i] < 5 for i in range(max(0, len(programs) + extra - RING))):
            round_()

    def send_item(order, spot):
        number = len(programs)
        programs.append(program(number, order, spot))
        stage.append(0)
        age.append(0)
        advance(number)

    def weight_gradient(height, own, far_, parts):
        base = len(programs)

        def copies(i, slot):
            return [
                pltpu.make_async_copy(own(i), left_in.at[slot, 0, pl.ds(0, height), :], lsem.at[slot]),
                pltpu.make_async_copy(far_(i), left_in.at[slot, 1, pl.ds(0, height), :], lsem.at[slot]),
            ]

        def body(i, slot):
            for right, far_right, factor, targets in parts:
                out = dot(left_in[slot, 0, :height, :], right()) + dot(left_in[slot, 1, :height, :], far_right())
                if factor != 1.0:
                    out = out * factor
                out = out.astype(BF16)
                for item, order, first in targets:
                    x = xs.at[(base + item) % XRING]
                    for pa in range(2):
                        for pb in range(2):
                            row = (pa * 2 + pb) * (height // 4) + first
                            block = out[row : row + 80, :]
                            if order[0] == "a":
                                x[lax.rem(pa + a, 2), i, pb] = block
                            else:
                                x[lax.rem(pb + b, 2), i, pa] = block

        streams(4, copies, body)

    def fetch(*pairs):
        copies = [pltpu.make_async_copy(x, y, local) for x, y in pairs]
        for copy in copies:
            copy.start()
        for copy in copies:
            copy.wait()

    def norm_back(source, gain, gain_at, layer, lowered):
        def copies(i, slot):
            return [pltpu.make_async_copy(source.at[tile(i, 64), :], rows_in.at[slot], lsem.at[slot])]

        def body(i, slot):
            at = tile(i, 64)
            values = rows_in[slot]
            center = values - jnp.mean(values, axis=-1, keepdims=True)
            s = lax.rsqrt(jnp.mean(center * center, axis=-1, keepdims=True) + EPSILON)
            unit = center * s
            grad = gh[at, :]
            e = grad * gain
            out = g[at, :] + s * (
                e - jnp.mean(e, axis=-1, keepdims=True) - unit * jnp.mean(e * unit, axis=-1, keepdims=True))
            g[at, :] = out
            sums[layer, pl.ds(gain_at, 1), :] += jnp.sum(grad * unit, axis=0, keepdims=True)
            sums[layer, pl.ds(gain_at + 1, 1), :] += jnp.sum(grad, axis=0, keepdims=True)
            if lowered:
                small = out.astype(BF16)
                low[0, at, :] = small
                sums[layer, pl.ds(4, 1), :] += jnp.sum(small.astype(F32), axis=0, keepdims=True)

        streams(8, copies, body)

    swaps = {}
    for layer in reversed(range(layers)):
        swaps[layer] = [
            net.push(active_t.at[layer, :, 1 - core], active_far.at[layer], to_core),
            net.push(hidden_t.at[layer], hidden_far.at[layer], to_core),
            net.push(context_t.at[layer], context_far.at[layer], to_core),
            net.push(normed_t.at[layer], normed_far.at[layer], to_core),
        ]
    fetch((cotangent, g))
    sums[...] = jnp.zeros_like(sums)

    for layer in reversed(range(layers)):
        vec = vectors.at[layer]

        @pl.loop(0, 8)
        def _(i):
            at = tile(i, 64)
            small = g[at, :].astype(BF16)
            low[0, at, :] = small
            sums[layer, pl.ds(7, 1), :] += jnp.sum(small.astype(F32), axis=0, keepdims=True)

        swap = net.push(low.at[0], grad_f_far.at[layer], to_core, swapped)
        swap.wait()
        fetch((grad_f_far.at[layer], low.at[1]))
        for copy in swaps[layer]:
            copy.wait_recv()

        def down_spot(half, column):
            def spot(pc, pa, pb):
                row = pc * 640 + (pa * 2 + pb) * 160 + half * 80
                return down_out.at[layer, pl.ds(pl.multiple_of(row, 16), 80), pl.ds(column * 640, 640)]
            return spot

        for column in range(2):
            room(2)
            weight_gradient(
                640, lambda i: active_t.at[layer, i, core], lambda i: active_far.at[layer, i],
                [(lambda column=column: low[0, :, column * 640 : column * 640 + 640],
                  lambda column=column: low[1, :, column * 640 : column * 640 + 640], 1.0,
                  [(0, "azb", 0), (1, "bza", 80)])],
            )
            send_item("azb", down_spot(0, column))
            send_item("bza", down_spot(1, column))
            if column == 0:
                round_()

        def copies_down(i, slot):
            return [
                pltpu.make_async_copy(down_full.at[layer, tile(i, 512), :], wide_w.at[slot], lsem.at[slot]),
                pltpu.make_async_copy(slopes.at[layer, :, tile(i, 512)], slope_in.at[slot], lsem.at[slot]),
            ]

        def body_down(i, slot):
            at = tile(i, 512)
            gh[:, :512] = dot(low[0], wide_w[slot], NT)

            @pl.loop(0, 8)
            def _(j):
                rows = tile(j, 64)
                small = (gh[rows, :512] * slope_in[slot, rows, :].astype(F32)).astype(BF16)
                gp[rows, at] = small
                sums[layer, pl.ds(8 + i, 1), :512] += jnp.sum(small.astype(F32), axis=0, keepdims=True)

        streams(10, copies_down, body_down)
        swap = net.push(gp.at[:, pl.ds(pl.multiple_of((1 - core) * 2560, 128), 2560)], grad_pre_far.at[layer], to_core,
                        swapped)
        round_()
        swap.wait()
        fetch((grad_pre_far.at[layer], gs))

        def up_spot(unit):
            def spot(pc, pa, pb):
                return up_out.at[layer, pl.ds(pl.multiple_of((pa * 2 + pb) * 80, 16), 80),
                                 pl.ds(pl.multiple_of(pc * 2560 + unit * 640, 128), 640)]
            return spot

        def rows_of(values, i):
            return values.at[layer, pl.ds(pl.multiple_of(i * 320, 16), 320), :]

        for pair in range(2):
            room(2)
            weight_gradient(
                320, lambda i: rows_of(hidden_t, i), lambda i: rows_of(hidden_far, i),
                [(lambda unit=unit: gp[:, pl.ds(pl.multiple_of(core * 2560 + unit * 640, 128), 640)],
                  lambda unit=unit: gs[:, unit * 640 : unit * 640 + 640], 1.0,
                  [(unit % 2, ("azb", "bza")[unit % 2], 0)]) for unit in (2 * pair, 2 * pair + 1)],
            )
            send_item("azb", up_spot(2 * pair))
            send_item("bza", up_spot(2 * pair + 1))
            if pair == 0:
                round_()

        def copies_up(i, slot):
            return [
                pltpu.make_async_copy(up_full.at[layer, tile(i, 256), pl.ds(k * 512, 512)],
                                      big.at[pl.ds(pl.multiple_of(slot * 2560 + k * 256, 256), 256), :], lsem.at[slot])
                for k in range(10)
            ]

        def body_up(i, slot):
            total_ = None
            for k in range(10):
                part = dot(gp[:, k * 512 : k * 512 + 512],
                           big[pl.ds(pl.multiple_of(slot * 2560 + k * 256, 256), 256), :], NT)
                total_ = part if total_ is None else total_ + part
            gh[:, tile(i, 256)] = total_

        streams(5, copies_up, body_up)
        round_()
        norm_back(middles.at[layer], vec[5:6, :], 5, layer, True)
        swap = net.push(low.at[0, :, pl.ds(pl.multiple_of((1 - core) * 640, 128), 640)], grad_o_far.at[layer], to_core,
                        swapped)

        def copies_out(i, slot):
            return [pltpu.make_async_copy(attn_full.at[layer, 3, tile(i, 256), :], wide_w.at[slot, pl.ds(0, 256), :],
                                          lsem.at[slot])]

        def body_out(i, slot):
            big[pl.ds(pl.multiple_of(3840 + i * 256, 256), 256), :] = dot(
                wide_w[slot, :256, :], low[0], NT).astype(BF16)

        streams(5, copies_out, body_out)
        swap.wait()
        fetch((grad_o_far.at[layer], low.at[1, :, pl.ds(0, 640)]), (lse_all.at[layer], lse))

        def small_spot(whole):
            def spot(pc, pa, pb):
                return whole.at[pl.ds(pl.multiple_of((pa * 2 + pb) * 80, 16), 80),
                                pl.ds(pl.multiple_of(pc * 640, 128), 640)]
            return spot

        room(1)
        weight_gradient(
            320, lambda i: rows_of(context_t, i), lambda i: rows_of(context_far, i),
            [(lambda: low[0, :, pl.ds(pl.multiple_of(core * 640, 128), 640)], lambda: low[1, :, :640], 1.0,
              [(0, "abz", 0)])],
        )
        send_item("abz", small_spot(out_out.at[layer]))
        round_()

        def copies_head(h, slot):
            at = pl.ds(pl.multiple_of(h * 80, 16), 80)
            return [
                pltpu.make_async_copy(qkv.at[layer, :, at, :], heads_in.at[slot, pl.ds(0, 3)], lsem.at[slot]),
                pltpu.make_async_copy(far.at[layer, :, at, :], heads_in.at[slot, pl.ds(3, 2)], lsem.at[slot]),
            ]

        def body_head(h, slot):
            at = pl.ds(pl.multiple_of(h * 80, 16), 80)
            at_k = pl.ds(pl.multiple_of(1280 + h * 80, 16), 80)
            at_v = pl.ds(pl.multiple_of(2560 + h * 80, 16), 80)
            query, norm = heads_in[slot, 0], lse[h]
            grad = big[pl.ds(pl.multiple_of(3840 + h * 80, 16), 80), :]
            halves, delta = [], None
            for k, v, mask, target in ((1, 2, 0, big.at[at_v, :]), (3, 4, 1, dfar.at[1, at, :])):
                p = jnp.exp(dot(heads_in[slot, k], query, TN) + masks[mask] - norm)
                dp = dot(heads_in[slot, v], grad, TN)
                part = jnp.sum(p * dp, axis=0, keepdims=True)
                delta = part if delta is None else delta + part
                target[...] = dot(grad, p.astype(BF16), NT).astype(BF16)
                halves.append((p, dp))
            total_ = None
            for (p, dp), k, target in zip(halves, (1, 3), (big.at[at_k, :], dfar.at[0, at, :])):
                ds = (p * (dp - delta)).astype(BF16)
                part = dot(heads_in[slot, k], ds)
                total_ = part if total_ is None else total_ + part
                target[...] = dot(query, ds, NT).astype(BF16)
            big[at, :] = total_.astype(BF16)

        for part in range(2):
            streams(8, lambda i, slot: copies_head(i + 8 * part, slot), lambda i, slot: body_head(i + 8 * part, slot))
            round_()
        swap = net.push(dfar, grad_kv_far.at[layer], to_core, swapped)
        swap.wait()

        def copies_far(i, slot):
            return [pltpu.make_async_copy(grad_kv_far.at[layer, :, tile(i, 128), :], far_in.at[slot], lsem.at[slot])]

        def body_far(i, slot):
            at = tile(i, 128)
            query = big[at, :].T
            gp[:, at] = query
            sums[layer, 2:3, at] = jnp.sum(query.astype(F32), axis=0, keepdims=True) * scale
            for which in range(2):
                rows = pl.ds(pl.multiple_of(1280 + which * 1280 + i * 128, 128), 128)
                both = (big[rows, :].astype(F32) + far_in[slot, which].astype(F32)).astype(BF16).T
                gp[:, pl.ds(pl.multiple_of(1280 + which * 1280 + i * 128, 128), 128)] = both
                if which == 1:
                    sums[layer, 3:4, at] = jnp.sum(both.astype(F32), axis=0, keepdims=True)

        streams(10, copies_far, body_far)
        swap = [
            net.push(gp.at[:, pl.ds(pl.multiple_of(t * 1280 + (1 - core) * 640, 128), 640)], grad_far.at[layer, t],
                     to_core, swapped)
            for t in range(3)
        ]
        for copy in swap:
            copy.wait()
        fetch(*[(grad_far.at[layer, t], gs.at[:, pl.ds(t * 640, 640)]) for t in range(3)])
        for group in ((0, 1), (2,)):
            room(len(group))
            weight_gradient(
                320, lambda i: rows_of(normed_t, i), lambda i: rows_of(normed_far, i),
                [(lambda t=t: gp[:, pl.ds(pl.multiple_of(t * 1280 + core * 640, 128), 640)],
                  lambda t=t: gs[:, t * 640 : t * 640 + 640], scale if t == 0 else 1.0,
                  [(t % 2, ("baz", "abz")[t % 2], 0)]) for t in group],
            )
            for t in group:
                send_item(("baz", "abz")[t % 2], small_spot(qkv_out.at[layer, t]))
            if len(group) == 2:
                round_()

        def copies_back(i, slot):
            return [pltpu.make_async_copy(attn_full.at[layer, i // 5, tile(i % 5, 256), :],
                                          wide_w.at[slot, pl.ds(0, 256), :], lsem.at[slot])]

        def body_back(i, slot):
            at = tile(i % 5, 256)
            out = dot(gp[:, pl.ds(pl.multiple_of((i // 5) * 1280, 128), 1280)], wide_w[slot, :256, :], NT)

            @pl.when(i < 5)
            def _():
                gh[:, at] = out * scale

            @pl.when(i >= 5)
            def _():
                gh[:, at] += out

        streams(15, copies_back, body_back)
        round_()
        norm_back(states.at[layer], vec[0:1, :], 0, layer, False)
        if layer > 0:
            round_()
    store = pltpu.make_async_copy(g, grad_out, local)
    store.start()
    while any(s < 7 for s in stage):
        round_()
    store.wait()
    net.drain()


def backward_all(cotangent, weights, kept, vectors, masks):
    any_ = pl.BlockSpec(memory_space=pl.ANY)
    vmem = pl.BlockSpec(memory_space=pltpu.VMEM)
    layers = vectors.shape[0]
    t = TOKENS

    def hbm(shape, dtype=BF16):
        return jax.ShapeDtypeStruct((layers,) + shape, dtype)

    out_shape = (
        jax.ShapeDtypeStruct((t, 1280), F32), hbm((1280, 1280)), hbm((320, 5120)), hbm((320, 1280)), hbm((3, 320, 1280)),
        hbm((24, 1280), F32),
        hbm((4, 640, t)), hbm((1280, t)), hbm((1280, t)), hbm((1280, t)), hbm((t, 1280)), hbm((t, 2560)), hbm((t, 640)),
        hbm((3, t, 640)), hbm((2, 1280, t)),
    )
    v = pltpu.VMEM
    items = ITEMS_A_LAYER * layers
    return pl.pallas_call(
        functools.partial(backward_kernel, layers),
        out_shape=out_shape,
        in_specs=[any_] * 14 + [vmem] * 2,
        out_specs=(any_,) * 5 + (vmem,) + (any_,) * 9,
        scratch_shapes=[
            v((t, 1280), F32), v((2, t, 1280), BF16), v((t, 5120), BF16), v((t, 2560), BF16), v((t, 1280), F32),
            v((2, 64, 1280), F32), v((5120, t), BF16), v((2, 1280, t), BF16), v((2, 5, 80, t), BF16), v((2, 2, 128, t), BF16),
            v((H, 1, t), F32), v((2, 512, 1280), BF16), v((2, t, 512), BF16), v((2, 2, 640, t), BF16),
            v((XRING, 2, 4, 2, 80, 640), BF16), v((RING, 4, 2, 80, 640), BF16), v((RING, 6, 80, 640), BF16),
            v((RING, 3, 80, 640), BF16), v((RING, 80, 640), BF16),
            pltpu.SemaphoreType.DMA, pltpu.SemaphoreType.DMA((2,)), pltpu.SemaphoreType.DMA,
            pltpu.SemaphoreType.DMA((RING, 4)), pltpu.SemaphoreType.DMA((RING,)), pltpu.SemaphoreType.DMA,
            pltpu.SemaphoreType.DMA((items * 12 + 12 * layers,)),
        ],
        compiler_params=pltpu.CompilerParams(collective_id=2, has_side_effects=True, vmem_limit_bytes=63 << 20),
        name="backward_all",
    )(cotangent, *weights, *kept, vectors, masks)


def total_kernel(values, out, held, got, sent, arrived):
    a, b, core, z = place()
    to_z = [device(a, b, core, lax.rem(z + s, 4)) for s in (1, 2, 3)]
    steps = [[device(a, b, 1 - core, z)], [device(a, 1 - b, core, z)], [device(1 - a, b, core, z)], to_z]
    greet([target for step in steps for target in step])
    net = Net(sent, arrived)
    held[0] = values[...]
    place_of = 0
    for number, step in enumerate(steps):
        first = place_of
        copies = []
        for target in step:
            copies.append(net.push(held.at[number], got.at[place_of], target))
            place_of += 1
        sum_ = held[number]
        for i, copy in enumerate(copies):
            copy.wait_recv()
            sum_ = sum_ + got[first + i]
        if number < 3:
            held[number + 1] = sum_
        else:
            out[...] = sum_
    net.drain()


def total(values):
    vmem = pl.BlockSpec(memory_space=pltpu.VMEM)
    return pl.pallas_call(
        total_kernel,
        out_shape=jax.ShapeDtypeStruct(values.shape, F32),
        in_specs=[vmem], out_specs=vmem,
        scratch_shapes=[
            pltpu.VMEM((4,) + values.shape, F32), pltpu.VMEM((6,) + values.shape, F32),
            pltpu.SemaphoreType.DMA, pltpu.SemaphoreType.DMA((6,)),
        ],
        compiler_params=pltpu.CompilerParams(collective_id=3, has_side_effects=True),
        name="total",
    )(values)


def plane_shards(
    inputs, lengths, cotangent, attn_gain, attn_shift, query_weight, query_bias, key_weight,
    value_weight, value_bias, out_weight, out_bias, mlp_gain, mlp_shift, up_weight, up_bias,
    down_weight, down_bias,
):
    a, b, core, z = place()
    layers = attn_gain.shape[0]
    block = inputs.shape[1]

    def gather_tokens(values):
        return jnp.concatenate(
            [send(pick(values, (z + step) % 2), "in%d" % step) for step in range(2)], axis=0
        )

    def return_tokens(values):
        got = [send(values[step * block : (step + 1) * block], "out%d" % step) for step in range(2)]
        got = jnp.stack(got)
        return jnp.stack([pick(got, (z + clip) % 2) for clip in range(2)])

    packed = jnp.concatenate(
        [attn_gain, attn_shift, query_bias, value_bias, out_bias, mlp_gain, mlp_shift, down_bias,
         up_bias], axis=1,
    )
    pieces = jnp.stack([packed] + [send(packed, "z%d" % s) for s in (1, 2, 3)])
    pieces = jnp.stack([pick(pieces, (z + 4 - from_z) % 4) for from_z in range(4)]).astype(F32)
    vectors = []
    for layer in range(layers):
        row = [pieces[:, layer, i * 320 : (i + 1) * 320].reshape(1280) for i in range(8)]
        row.append(pieces[:, layer, 2560:].reshape(5120))
        vectors.append(tuple(row))

    state = gather_tokens(inputs).astype(F32)

    far_lengths = send(lengths, "core")
    four = jnp.where(core == 0, jnp.concatenate([lengths, far_lengths]),
                     jnp.concatenate([far_lengths, lengths]))
    length = pick(four, z)

    def positions(which):
        return jnp.concatenate(
            [(2 * which + (z + step) % 2) * block + jnp.arange(block) for step in range(2)]
        )

    def mask_of(which):
        return jnp.where(positions(which) < length, 0.0, NEGATIVE).astype(F32)[:, None]

    masks = (mask_of(core), mask_of(1 - core))

    table = jnp.zeros((layers, 24, 1280), F32)
    for layer in range(layers):
        rows = jnp.stack(vectors[layer][:8])
        wide = jnp.pad(vectors[layer][8].reshape(10, 512), ((0, 0), (0, 768)))
        table = table.at[layer, :18].set(jnp.concatenate([rows, wide]))
    attn = jnp.stack([query_weight, key_weight, value_weight, out_weight], axis=1)
    (attn, up, down, normed_t, qkv, far, lse, context_t, middles, hidden_t, slopes, active_t, states) = forward_all(
        state, attn, up_weight, down_weight, table, jnp.stack(masks)
    )
    state = states[layers]
    output = return_tokens(state.astype(BF16))

    row_mask = (positions(core) < length).astype(F32)
    grad = gather_tokens(cotangent).astype(F32) * row_mask[:, None]
    lse_mask = jnp.stack(masks)
    results = backward_all(
        grad, (attn, up, down),
        (normed_t, qkv, far, lse, context_t, middles, hidden_t, slopes, active_t.reshape(layers, 4, 2, 640, -1), states),
        table, lse_mask,
    )
    grad, down_grad, up_grad, out_grad, qkv_grad, small = results[:6]
    input_grad = return_tokens(grad.astype(BF16)).astype(F32)
    small = jnp.concatenate([small[:, :8].reshape(layers, -1), small[:, 8:18, :512].reshape(layers, -1)], axis=1)
    sums = total(small.reshape(-1, 128)).reshape(layers, -1)
    vec = pick(sums[:, :10240].reshape(layers, 8, 4, 320), z, 2)
    up_bias_grad = pick(sums[:, 10240:].reshape(layers, 4, 1280), z, 1)

    query_grad, key_grad, value_grad = [qkv_grad[:, i].astype(F32) for i in range(3)]
    out_grad, up_grad, down_grad = out_grad.astype(F32), up_grad.astype(F32), down_grad.astype(F32)
    return (
        output, input_grad, vec[:, 0], vec[:, 1], query_grad, vec[:, 2], key_grad, value_grad,
        vec[:, 3], out_grad, vec[:, 4], vec[:, 5], vec[:, 6], up_grad, up_bias_grad, down_grad,
        vec[:, 7],
    )


def pick_body(mesh):
    if mesh.shape["rep"] == 8 and mesh.shape["shard"] == 4:
        return plane_shards
    return general_shards


def solution(mesh):
    body = pick_body(mesh)
    placed = (
        P("rep", "shard", None),
        P("rep"),
        P("rep", "shard", None),
        P(None, "shard"),
        P(None, "shard"),
        P(None, "shard", None),
        P(None, "shard"),
        P(None, "shard", None),
        P(None, "shard", None),
        P(None, "shard"),
        P(None, "shard", None),
        P(None, "shard"),
        P(None, "shard"),
        P(None, "shard"),
        P(None, "shard", None),
        P(None, "shard"),
        P(None, "shard", None),
        P(None, "shard"),
    )
    return jax.shard_map(
        body,
        mesh=mesh,
        in_specs=placed,
        out_specs=(
            P("rep", "shard", None),
            P("rep", "shard", None),
            P(None, "shard"),
            P(None, "shard"),
            P(None, "shard", None),
            P(None, "shard"),
            P(None, "shard", None),
            P(None, "shard", None),
            P(None, "shard"),
            P(None, "shard", None),
            P(None, "shard"),
            P(None, "shard"),
            P(None, "shard"),
            P(None, "shard", None),
            P(None, "shard"),
            P(None, "shard", None),
            P(None, "shard"),
        ),
        check_vma=False,
    )
```

profile of v0, /device:TPU:11, one launch (start us, length us, event | category | flops | bytes accessed | tf_op | source)
XLA Modules:
  0.0 1133.7 jit_solution(961954315010001898)
XLA Ops:
  0.7 0.9 concatenate.65
  1.6 0.2 collective-permute-start.4
  1.8 2.3 collective-permute-start.3
  4.1 2.2 collective-permute-start.2
  6.3 1.5 collective-permute-start.5
  7.8 2.6 dynamic-slice_bitcast_fusion.3
  10.4 2.4 collective-permute-start
  12.9 2.4 dynamic-slice_bitcast_fusion.1
  15.4 5.3 pad_maximum_fusion.refs_1_
  20.7 0.2 collective-permute-start.1
  21.0 0.6 dynamic_slice.56
  21.6 0.6 compare_select_fusion
  22.2 0.1 copy.60
  22.4 0.1 copy.59
  22.5 0.8 pad_maximum_fusion.2.refs_5_.refs_15_
  23.4 0.7 fusion.4
  24.1 4.3 collective-permute-start.8
  28.4 2.2 collective-permute-start.9
  30.6 0.1 pad_maximum_fusion.4
  30.8 0.1 maximum_convert_fusion.2
  31.0 0.2 convert_reduce_fusion.5
  31.1 0.1 stack_reshape_squeeze.59
  31.2 0.1 stack_reshape_squeeze.58
  31.3 0.1 stack_reshape_squeeze.57
  31.5 0.2 convert_reduce_fusion.13
  31.6 0.1 stack_reshape_squeeze.51
  31.9 0.1 stack_reshape_squeeze.48
  32.0 0.2 convert_reduce_fusion.9
  32.1 0.1 stack_reshape_squeeze.55
  32.2 0.1 stack_reshape_squeeze.54
  32.5 0.2 convert_reduce_fusion.1
  32.7 0.1 stack_reshape_squeeze.63
  33.3 1.1 scatter.9.refs_4_.refs_14_
  34.5 14.2 %collective-permute-done.1 = bf16[256,1280]{1,0:T(8,128)(2,1)S(1)} collective-permute-done((bf16[256,1280]{1,0:T(8,128)(2,1)}, bf16[256,1280]{1,0:T(8,128)(2,1)S(1)}, u32[]{:S(2)}, u32[]{:S(2)}) %collective-permute-start.1) | collective-permute-done | bytes 655392 | tf_op jit(solution)/shard_map/ppermute | solution.py:459
  48.7 2.8 maximum_convert_fusion.refs_0_
  51.4 316.0 %forward_all.1 = (bf16[2,4,1280,1280]{3,2,1,0:T(8,128)(2,1)}, bf16[2,1280,5120]{2,1,0:T(8,128)(2,1)}, bf16[2,5120,1280]{2,1,0:T(8,128)(2,1)}, bf16[2,1280,512]{2...) custom-call(f32[512,1280]{1,0:T(8,128)} %maximum_convert_fusion.refs, ...), custom_call_target="tpu_custom_call" | custom-call | tf_op jit(solution)/shard_map/forward_all/pallas_call | solution.py:814
  367.5 5.5 convert.6
  373.0 2.8 convert_multiply_fusion.refs_0_
  375.8 666.4 %backward_all.1 = (f32[512,1280]{1,0:T(8,128)}, bf16[2,1280,1280]{2,1,0:T(8,128)(2,1)}, bf16[2,320,5120]{2,1,0:T(8,128)(2,1)}, bf16[2,320,1280]{2,1,0:T(8,128)(2...) custom-call(f32[512,1280]{1,0:T(8,128)} %convert_multiply_fusion.ref, ...), custom_call_target="tpu_custom_call" | custom-call | tf_op jit(solution)/shard_map/backward_all/pallas_call | solution.py:1289
  1042.2 1.0 slice_bitcast_fusion.3
  1043.2 0.9 slice_bitcast_fusion.2
  1044.3 0.7 reshape.209.values
  1045.0 22.5 %total.1 = f32[240,128]{1,0:T(8,128)} custom-call(f32[240,128]{1,0:T(8,128)} %reshape.209.values), custom_call_target="tpu_custom_call" | custom-call | tf_op jit(solution)/shard_map/total/pallas_call | solution.py:1336
  1067.5 1.0 reshape.210
  1068.5 2.2 slice_bitcast_fusion
  1070.8 0.1 convert_element_type.58
  1070.9 0.1 fusion.5
  1071.0 0.1 reshape.211
  1071.2 2.2 collective-permute-start.11
  1073.5 4.1 collective-permute-start.10
  1077.6 2.7 collective-permute-start.7
  1080.3 2.8 collective-permute-start.6
  1083.1 7.2 bitcast_convert_fusion
  1090.4 2.0 convert_element_type.66
  1092.4 6.8 convert_element_type.67
  1099.1 6.0 convert_element_type.68
  1105.1 0.6 dynamic-slice_bitcast_fusion.4
  1105.7 0.6 slice_bitcast_fusion.4
  1106.3 1.8 fusion.1
  1108.1 15.9 %collective-permute-done.7 = bf16[256,1280]{1,0:T(8,128)(2,1)S(1)} collective-permute-done((bf16[256,1280]{1,0:T(8,128)(2,1)S(1)}, bf16[256,1280]{1,0:T(8,128)(2,1)S(1)}, u32[]{:S(2)}, u32[]{:S(2)}) %collective-permute-start.7) | collective-permute-done | bytes 655392 | tf_op jit(solution)/shard_map/ppermute | solution.py:459
  1124.0 6.2 collective-permute-done.6
  1130.2 0.5 fusion.3
  1130.7 1.2 pad_maximum_fusion.1
  1131.8 1.7 maximum_convert_fusion.1
  (66 shorter events, 1.5 us)
Async XLA Ops:
  1.6 22.5 %collective-permute-start.4 = (bf16[2,3840]{1,0:T(2,128)(2,1)S(1)}, bf16[2,3840]{1,0:T(2,128)(2,1)S(1)}, u32[]{:S(2)}, u32[]{:S(2)}) collective-permute-start(bf16[2,3840]{1,0:T(2,128)(2,1)S(1)} %concatenate.65), channel_id=1, source_target_pairs={{0,3},{1,0},{2,1},{3,2},{4,7},{5,4},{6,5},{7,6},{8,11},{9,8},{10,9... | collective-permute-start | bytes 46088 | tf_op jit(solution)/shard_map/ppermute | solution.py:459
  1.8 26.6 %collective-permute-start.3 = (bf16[2,3840]{1,0:T(2,128)(2,1)S(1)}, bf16[2,3840]{1,0:T(2,128)(2,1)S(1)}, u32[]{:S(2)}, u32[]{:S(2)}) collective-permute-start(bf16[2,3840]{1,0:T(2,128)(2,1)S(1)} %concatenate.65), channel_id=1, source_target_pairs={{0,2},{1,3},{2,0},{3,1},{4,6},{5,7},{6,4},{7,5},{8,10},{9,11},{10,... | collective-permute-start | bytes 46088 | tf_op jit(solution)/shard_map/ppermute | solution.py:459
  4.1 26.5 %collective-permute-start.2 = (bf16[2,3840]{1,0:T(2,128)(2,1)S(1)}, bf16[2,3840]{1,0:T(2,128)(2,1)S(1)}, u32[]{:S(2)}, u32[]{:S(2)}) collective-permute-start(bf16[2,3840]{1,0:T(2,128)(2,1)S(1)} %concatenate.65), channel_id=1, source_target_pairs={{0,1},{1,2},{2,3},{3,0},{4,5},{5,6},{6,7},{7,4},{8,9},{9,10},{10,1... | collective-permute-start | bytes 46088 | tf_op jit(solution)/shard_map/ppermute | solution.py:459
  6.3 14.4 %collective-permute-start.5 = (s32[2]{0:T(128)}, s32[2]{0:T(128)S(1)}, u32[]{:S(2)}, u32[]{:S(2)}) collective-permute-start(s32[2]{0:T(128)} %param.23), channel_id=1, source_target_pairs={{0,4},{1,5},{2,6},{3,7},{4,0},{5,1},{6,2},{7,3},{8,12},{9,13},{10,... | collective-permute-start | bytes 32 | tf_op jit(solution)/shard_map/ppermute | solution.py:459
  7.8 7.5 copy-start.2
  7.8 7.6 copy-start.3
  10.4 24.1 %collective-permute-start = (bf16[256,1280]{1,0:T(8,128)(2,1)}, bf16[256,1280]{1,0:T(8,128)(2,1)}, u32[]{:S(2)}, u32[]{:S(2)}) collective-permute-start(bf16[256,1280]{1,0:T(8,128)(2,1)} %get-tuple-element.108), channel_id=1, source_target_pairs={{0,0},{1,1},{2,4},{3,5},{4,2},{5,3},{6,6},{7,7},{8,8},{9,9},{10,12... | collective-permute-start | bytes 1966088 | tf_op jit(solution)/shard_map/ppermute | solution.py:459
  15.4 5.5 copy-start.7
  20.7 28.0 %collective-permute-start.1 = (bf16[256,1280]{1,0:T(8,128)(2,1)}, bf16[256,1280]{1,0:T(8,128)(2,1)S(1)}, u32[]{:S(2)}, u32[]{:S(2)}) collective-permute-start(bf16[256,1280]{1,0:T(8,128)(2,1)} %get-tuple-element.109), channel_id=1, source_target_pairs={{0,1},{1,0},{2,5},{3,4},{4,3},{5,2},{6,7},{7,6},{8,9},{9,8},{10,13... | collective-permute-start | bytes 1966088 | tf_op jit(solution)/shard_map/ppermute | solution.py:459
  24.1 348.9 %collective-permute-start.8 = (bf16[256,1280]{1,0:T(8,128)(2,1)}, bf16[256,1280]{1,0:T(8,128)(2,1)S(1)}, u32[]{:S(2)}, u32[]{:S(2)}) collective-permute-start(bf16[256,1280]{1,0:T(8,128)(2,1)} %get-tuple-element.104), channel_id=1, source_target_pairs={{0,0},{1,1},{2,4},{3,5},{4,2},{5,3},{6,6},{7,7},{8,8},{9,9},{10,12... | collective-permute-start | bytes 1966088 | tf_op jit(solution)/shard_map/ppermute | solution.py:459
  28.4 344.6 %collective-permute-start.9 = (bf16[256,1280]{1,0:T(8,128)(2,1)}, bf16[256,1280]{1,0:T(8,128)(2,1)}, u32[]{:S(2)}, u32[]{:S(2)}) collective-permute-start(bf16[256,1280]{1,0:T(8,128)(2,1)} %get-tuple-element.105), channel_id=1, source_target_pairs={{0,1},{1,0},{2,5},{3,4},{4,3},{5,2},{6,7},{7,6},{8,9},{9,8},{10,13... | collective-permute-start | bytes 1966088 | tf_op jit(solution)/shard_map/ppermute | solution.py:459
  34.4 17.0 %copy-start.1 = (f32[2,24,1280]{2,1,0:T(8,128)}, f32[2,24,1280]{2,1,0:T(8,128)S(1)}, u32[]{:S(2)}) copy-start(f32[2,24,1280]{2,1,0:T(8,128)S(1)} %scatter.9.refs_4_.refs_14_) | copy-start | bytes 737284
  1042.2 28.5 %copy-start = (f32[512,1280]{1,0:T(8,128)S(1)}, f32[512,1280]{1,0:T(8,128)}, u32[]{:S(2)}) copy-start(f32[512,1280]{1,0:T(8,128)} %get-tuple-element.73) | copy-start | bytes 7864324
  1068.5 2.4 copy-start.6
  1070.9 6.7 copy-start.5
  1071.2 35.1 %collective-permute-start.11 = (bf16[256,1280]{1,0:T(8,128)(2,1)S(1)}, bf16[256,1280]{1,0:T(8,128)(2,1)}, u32[]{:S(2)}, u32[]{:S(2)}) collective-permute-start(bf16[256,1280]{1,0:T(8,128)(2,1)S(1)} %get-tuple-element.102), channel_id=1, source_target_pairs={{1,0},{0,1},{5,2},{4,3},{3,4},{2,5},{7,6},{6,7},{9,8},{8,9},{13,10... | collective-permute-start | bytes 1966088 | tf_op jit(solution)/shard_map/ppermute | solution.py:459
  1073.5 32.9 %collective-permute-start.10 = (bf16[256,1280]{1,0:T(8,128)(2,1)S(1)}, bf16[256,1280]{1,0:T(8,128)(2,1)}, u32[]{:S(2)}, u32[]{:S(2)}) collective-permute-start(bf16[256,1280]{1,0:T(8,128)(2,1)S(1)} %get-tuple-element.103), channel_id=1, source_target_pairs={{0,0},{1,1},{4,2},{5,3},{2,4},{3,5},{6,6},{7,7},{8,8},{9,9},{12,10... | collective-permute-start | bytes 1966088 | tf_op jit(solution)/shard_map/ppermute | solution.py:459
  1077.6 46.3 %collective-permute-start.7 = (bf16[256,1280]{1,0:T(8,128)(2,1)S(1)}, bf16[256,1280]{1,0:T(8,128)(2,1)S(1)}, u32[]{:S(2)}, u32[]{:S(2)}) collective-permute-start(bf16[256,1280]{1,0:T(8,128)(2,1)S(1)} %copy-done.5), channel_id=1, source_target_pairs={{1,0},{0,1},{5,2},{4,3},{3,4},{2,5},{7,6},{6,7},{9,8},{8,9},{13,10... | collective-permute-start | bytes 1966088 | tf_op jit(solution)/shard_map/ppermute | solution.py:459
  1080.3 49.9 %collective-permute-start.6 = (bf16[256,1280]{1,0:T(8,128)(2,1)S(1)}, bf16[256,1280]{1,0:T(8,128)(2,1)S(1)}, u32[]{:S(2)}, u32[]{:S(2)}) collective-permute-start(bf16[256,1280]{1,0:T(8,128)(2,1)S(1)} %get-tuple-element.99), channel_id=1, source_target_pairs={{0,0},{1,1},{4,2},{5,3},{2,4},{3,5},{6,6},{7,7},{8,8},{9,9},{12,10... | collective-permute-start | bytes 1966088 | tf_op jit(solution)/shard_map/ppermute | solution.py:459
  1083.1 9.2 slice-start.2
  1083.1 7.3 copy-start.4
  1083.1 9.2 slice-start.3
  1090.4 8.7 slice-start
  1092.4 6.8 slice-start.1
  1099.1 6.0 slice-start.4
where the time goes:
time: 1150 us; the launch traced here: 1130 us
  Pallas kernels  1000 us (87%)
  other arithmetic  46.8 us (4%)
  waiting for transfers between devices  36.3 us (3%)
  starting transfers between devices  27.3 us (2%)
  local copies, waits for them, and re-layouts  17.1 us (1%)
    pallas_call x1, Pallas kernels, backward_all(): pl.pallas_call(functools.partial(backward_kernel, layers), out_shape=out_...  666 us
    pallas_call x1, Pallas kernels, forward_all(): pl.pallas_call(functools.partial(forward_kernel, layers), out_shape=out_s...  316 us
    ppermute x12, waiting for transfers between devices, send(): return lax.ppermute(values, BOTH, PAIRS[way])  36.3 us
    ppermute x12, starting transfers between devices, send(): return lax.ppermute(values, BOTH, PAIRS[way])  27.3 us
  transfers between devices with their start and end apart: 12, of which 3 were waited for; matrix products, arithmetic and copies ran while one was open for 4% of the time, Pallas kernels for 28%

commit v1 on v0

--- a/solution.py
+++ b/solution.py
@@ -1,4 +1,5 @@
 import functools
+import itertools
 import math
 
 import jax
@@ -425,40 +426,6 @@
     )
 
 
-def device_index(a, b, core, z):
-    return ((a * 2 + b) * 2 + core) * 4 + z
-
-
-def make_pairs(target):
-    return [
-        (device_index(a, b, core, z), device_index(*target(a, b, core, z)))
-        for a in range(2)
-        for b in range(2)
-        for core in range(2)
-        for z in range(4)
-    ]
-
-
-PAIRS = {
-    "a": make_pairs(lambda a, b, c, z: (1 - a, b, c, z)),
-    "b": make_pairs(lambda a, b, c, z: (a, 1 - b, c, z)),
-    "ab": make_pairs(lambda a, b, c, z: (1 - a, 1 - b, c, z)),
-    "core": make_pairs(lambda a, b, c, z: (a, b, 1 - c, z)),
-    "z1": make_pairs(lambda a, b, c, z: (a, b, c, (z + 1) % 4)),
-    "z2": make_pairs(lambda a, b, c, z: (a, b, c, (z + 2) % 4)),
-    "z3": make_pairs(lambda a, b, c, z: (a, b, c, (z + 3) % 4)),
-}
-for step in range(2):
-    PAIRS["in%d" % step] = make_pairs(
-        lambda a, b, c, z, step=step: (a, b, z // 2, 2 * c + (z + step) % 2)
-    )
-    PAIRS["out%d" % step] = [(target, source) for source, target in PAIRS["in%d" % step]]
-
-
-def send(values, way):
-    return lax.ppermute(values, BOTH, PAIRS[way])
-
-
 def pick(values, index, axis=0):
     return lax.dynamic_index_in_dim(values, index, axis, keepdims=False)
 
@@ -466,10 +433,6 @@
 def place():
     rep = lax.axis_index("rep")
     return rep // 4, (rep // 2) % 2, rep % 2, lax.axis_index("shard")
-
-
-def after(values, *others):
-    return lax.optimization_barrier((values,) + others)[0]
 
 
 MESH = pl.DeviceIdType.MESH
@@ -496,11 +459,67 @@
         for copy in self.copies:
             copy.wait_send()
 
-def greet(targets):
+def greet(targets, regroup=None):
     barrier = pltpu.get_barrier_semaphore()
+
+    def signal(target):
+        pl.semaphore_signal(barrier, inc=1, device_id=target, device_id_type=MESH)
+
     for target in targets:
-        pl.semaphore_signal(barrier, inc=1, device_id=target, device_id_type=MESH)
-    pl.semaphore_wait(barrier, len(targets))
+        signal(target)
+    if regroup is None:
+        pl.semaphore_wait(barrier, len(targets))
+        return
+    stays, to, source, both = regroup
+    for step in range(2):
+        for target in (source[step], to[step]) if both else (source[step],):
+
+            @pl.when(True if step else jnp.logical_not(stays))
+            def _():
+                signal(target)
+
+    extra = 2 if both else 1
+
+    @pl.when(stays)
+    def _():
+        pl.semaphore_wait(barrier, len(targets) + extra)
+
+    @pl.when(jnp.logical_not(stays))
+    def _():
+        pl.semaphore_wait(barrier, len(targets) + 2 * extra)
+
+
+def regrouping():
+    a, b, core, z = place()
+    to, source = [], []
+    for step in range(2):
+        to.append(device(a, b, z // 2, 2 * core + lax.rem(z + step, 2)))
+        source.append(device(a, b, z // 2, 2 * core + lax.rem(z + step, 2)))
+    return core == z // 2, to, source
+
+
+class Swap:
+    def __init__(self, net, source, target_ref, target, stays, sent, local):
+        self.stays = stays
+        self.far = pltpu.make_async_remote_copy(
+            src_ref=source, dst_ref=target_ref, send_sem=sent, recv_sem=net.arrived.at[net.count],
+            device_id=target, device_id_type=MESH)
+        self.near = pltpu.make_async_copy(source, target_ref, local) if stays is not None else None
+        net.count += 1
+
+    def both(self, near, far):
+        if self.stays is None:
+            far()
+            return
+        pl.when(self.stays)(near)
+        pl.when(jnp.logical_not(self.stays))(far)
+
+    def start(self):
+        self.both(lambda: self.near.start(), lambda: self.far.start())
+        return self
+
+    def wait(self):
+        self.both(lambda: self.near.wait(), lambda: self.far.wait())
 
 def gather_regions(index, zs, chip, core):
     part = chip * 2 + core
@@ -562,7 +581,15 @@
         return whose[which].at[index // 6].at[at]
 
     def start(index):
-        return [net.push(refs_at(index, 0, a, b, shards), refs_at(index, z, a, b, outs), to_z[s]) for s in (1, 2, 3)]
+        if index % 6 > 1:
+            return [[net.push(refs_at(index, 0, a, b, shards), refs_at(index, z, a, b, outs), to_z[s])] for s in (1, 2, 3)]
+        here, there = [
+            pl.ds(pl.multiple_of(zs * 320 + ((a * 2 + b) * 2 + core) * 40, 8), 40) for zs in (0, z)]
+        return [
+            [net.push(shards[0][i].at[index // 6, here, :], outs[0].at[index // 6, i, there, :], to_z[s])
+             for i in (2 * (index % 6), 2 * (index % 6) + 1)]
+            for s in (1, 2, 3)
+        ]
 
     def on(index, s, pa, pb, target):
         ref = refs_at(index, behind[s], pa, pb, outs)
@@ -573,11 +600,12 @@
 
     def own_copies(step):
         layer, which = step // 3, step % 3
-        shard, out = shards[which].at[layer], outs[which].at[layer]
+        out = outs[which].at[layer]
+        shard = shards[which].at[layer] if which else None
         ins, back = [], []
         for i in range(4):
             if which == 0:
-                source, target = shard.at[i], out.at[i, pl.ds(pl.multiple_of(z * 320, 8), 320), :]
+                source, target = shards[0][i].at[layer], out.at[i, pl.ds(pl.multiple_of(z * 320, 8), 320), :]
             elif which == 1:
                 source = shard.at[:, pl.ds(i * 1280, 1280)]
                 target = out.at[pl.ds(pl.multiple_of(z * 320, 8), 320), pl.ds(i * 1280, 1280)]
@@ -604,7 +632,8 @@
         if t < count:
             mid[t] = {}
             for s in (1, 2, 3):
-                zed[t][s - 1].wait_recv()
+                for copy in zed[t][s - 1]:
+                    copy.wait_recv()
                 mid[t][s] = (on(t, s, a, b, to_b), on(t, s, a, b, to_a))
                 on(t, s, a, b, to_core)
             if t + 2 < count:
@@ -657,23 +686,62 @@
 
 
 def forward_kernel(layers, *refs):
-    (tokens, attn, up, down, vectors, masks,
+    (tokens, cotangent, query_w, key_w, value_w, out_w, up, down, part, lengths,
      attn_full, up_full, down_full, keep_normed, keep_qkv, keep_far, keep_lse, keep_context, keep_middle,
-     keep_hidden, keep_slope, keep_active, states,
+     keep_hidden, keep_slope, keep_active, states, far_active, far_hidden, far_context, far_normed,
+     cotangent_in, final, vectors, masks,
      state, middle, normed, normed_t, hidden_t, qkv, far, context_t, context, active, active_t, slope, lse,
-     small_w, up_w, down_w, copies, product,
-     local, wsem, saved, swapped, sent, arrived) = refs
+     small_w, up_w, down_w, copies, product, parts_in, lengths_in,
+     local, wsem, saved, swapped, handed, early, moved, stayed, sent, arrived) = refs
     a, b, core, z = place()
     to_core = device(a, b, 1 - core, z)
-    greet([device(a, b, core, lax.rem(z + s, 4)) for s in (1, 2, 3)]
-          + [device(1 - a, b, core, z), device(a, 1 - b, core, z), to_core])
+    to_z = [device(a, b, core, lax.rem(z + s, 4)) for s in (1, 2, 3)]
+    stays, to, source = regrouping()
+    greet(to_z + [device(1 - a, b, core, z), device(a, 1 - b, core, z), to_core], (stays, to, source, False))
     net = Net(sent, arrived)
-    load = pltpu.make_async_copy(tokens, state, local)
-    load.start()
-    load.wait()
-    ticks = gather_program(net, layers, (attn, up, down), (attn_full, up_full, down_full), copies, local)
+
+    def regroup(values, targets, first):
+        return [
+            Swap(net, values.at[lax.rem(z + step, 2)], targets[step], to[step], None if step else stays,
+                 moved.at[first + step], stayed.at[first]).start()
+            for step in range(2)
+        ]
+
+    shared = [net.push(part, parts_in.at[i], to_z[i], early) for i in range(3)]
+    shared.append(net.push(lengths, lengths_in, to_core, early))
+    ticks = gather_program(net, layers, ((query_w, key_w, value_w, out_w), up, down), (attn_full, up_full, down_full),
+                           copies, local)
     twin = next(ticks)
     clock = [-1]
+    block = tokens.shape[1]
+    tokens_here = regroup(tokens, [context.at[pl.ds(step * block, block), :] for step in range(2)], 0)
+    next(ticks)
+    next(ticks)
+    clock[0] = 1
+    for copy in shared:
+        copy.wait()
+
+    @pl.loop(0, layers)
+    def _(i):
+        total_ = part[i].astype(F32)
+        for j in range(3):
+            total_ = total_ + parts_in[j, i].astype(F32)
+        vectors[i] = total_
+
+    which = lax.rem(z, 2)
+    length = jnp.where(z // 2 == core, lengths[which], lengths_in[which])[0:1, 0:1]
+    for i in range(2):
+        owner = core if i == 0 else 1 - core
+        for step in range(2):
+            first = (2 * owner + lax.rem(z + step, 2)) * block
+            at = (lax.broadcasted_iota(jnp.int32, (block, 1), 0) + first).astype(F32)
+            masks[i, step * block : (step + 1) * block, :] = jnp.where(at < length, 0.0, NEGATIVE)
+    for copy in tokens_here:
+        copy.wait()
+
+    @pl.loop(0, 8)
+    def _(i):
+        state[tile(i, 64), :] = context[tile(i, 64), :].astype(F32)
 
     def pump(until):
         while clock[0] < until:
@@ -693,9 +761,19 @@
         copy.start()
         saves.append(copy)
 
+    given, taken = [], []
+
+    def hand(source, target):
+        copy = net.push(source, target, to_core, handed)
+        given.append(copy)
+        taken.append(copy)
+
     scale = float(80) ** (-0.5)
     for layer in range(layers):
         base = 6 * layer
+        for copy in given:
+            copy.wait_send()
+        given.clear()
         vec = vectors.at[layer]
 
         def row(i):
@@ -706,6 +784,7 @@
         normalize_rows(state, normed, row(0), row(1))
         transpose_into(normed_t, normed, 1280)
         save(normed_t, keep_normed.at[layer])
+        hand(normed_t, far_normed.at[layer])
         ready(base, base + 1)
 
         def project(which, bias, factor, target):
@@ -731,11 +810,15 @@
         for part in range(4):
             if part == 2:
                 pump(base + 5)
+                if layer == layers - 1:
+                    cotangent_at = [copies.at[step, pl.ds(0, block), :] for step in range(2)]
+                    cotangent_here = regroup(cotangent, cotangent_at, 2)
             attend_heads(4 * part, 4 * part + 4, qkv.at[0], qkv.at[1], qkv.at[2], far.at[layer], masks, context_t, lse)
         save(qkv, keep_qkv.at[layer])
         save(far.at[layer], keep_far.at[layer])
         save(lse, keep_lse.at[layer])
         save(context_t, keep_context.at[layer])
+        hand(context_t, far_context.at[layer])
 
         @pl.loop(0, 10)
         def _(i):
@@ -753,6 +836,7 @@
         normalize_rows(middle, normed, row(5), row(6))
         transpose_into(hidden_t, normed, 1280)
         save(hidden_t, keep_hidden.at[layer])
+        hand(hidden_t, far_hidden.at[layer])
         pump(base + 6)
         ready(base + 2, base + 3)
 
@@ -776,6 +860,9 @@
         stream(10, copy_up, body_up)
         save(slope, keep_slope.at[layer])
         save(active_t, keep_active.at[layer])
+        for i in range(4):
+            rows = pl.ds(pl.multiple_of(i * 1280 + (1 - core) * 640, 128), 640)
+            hand(active_t.at[rows, :], far_active.at[layer, i])
         ready(base + 4, base + 5)
 
         def copy_down(i, slot):
@@ -790,16 +877,29 @@
             state[:, at] = middle[:, at] + dot(active[...], down_w[slot]) + vec[7:8, at]
 
         stream(5, copy_down, body_down)
-    save(state, states.at[layers])
+
+    @pl.loop(0, 8)
+    def _(i):
+        normed[tile(i, 64), :] = state[tile(i, 64), :].astype(BF16)
+
+    for copy in cotangent_here:
+        copy.wait()
+    save(normed, final)
+    for step in range(2):
+        save(cotangent_at[step], cotangent_in.at[step])
     for copy in saves:
         copy.wait()
+    for copy in given:
+        copy.wait_send()
+    for copy in taken:
+        copy.wait_recv()
     net.drain()
 
 
-def forward_all(tokens, attn, up, down, vectors, masks):
+def forward_all(tokens, cotangent, shards, part, lengths):
     any_ = pl.BlockSpec(memory_space=pl.ANY)
     vmem = pl.BlockSpec(memory_space=pltpu.VMEM)
-    layers = up.shape[0]
+    layers = part.shape[0]
     t = TOKENS
 
     def hbm(shape, dtype=BF16):
@@ -808,26 +908,30 @@
     out_shape = (
         hbm((4, 1280, 1280)), hbm((1280, 5120)), hbm((5120, 1280)),
         hbm((1280, t)), hbm((3, 1280, t)), hbm((2, 1280, t)), hbm((H, 1, t), F32), hbm((1280, t)), hbm((t, 1280), F32),
-        hbm((1280, t)), hbm((t, 5120)), hbm((5120, t)), jax.ShapeDtypeStruct((layers + 1, t, 1280), F32),
+        hbm((1280, t)), hbm((t, 5120)), hbm((5120, t)), hbm((t, 1280), F32),
+        hbm((4, 640, t)), hbm((1280, t)), hbm((1280, t)), hbm((1280, t)),
+        jax.ShapeDtypeStruct(tokens.shape, BF16), jax.ShapeDtypeStruct((t, 1280), BF16), hbm((24, 1280), F32), jax.ShapeDtypeStruct((2, t, 1), F32),
     )
     v = pltpu.VMEM
     return pl.pallas_call(
         functools.partial(forward_kernel, layers),
         out_shape=out_shape,
-        in_specs=[any_] * 4 + [vmem] * 2,
-        out_specs=(any_,) * len(out_shape),
+        in_specs=[any_] * 8 + [vmem] * 2,
+        out_specs=(any_,) * (len(out_shape) - 2) + (vmem,) * 2,
         scratch_shapes=[
             v((t, 1280), F32), v((t, 1280), F32), v((t, 1280), BF16), v((1280, t), BF16), v((1280, t), BF16),
             v((3, 1280, t), BF16), v((layers, 2, 1280, t), BF16), v((1280, t), BF16), v((t, 1280), BF16),
             v((t, 5120), BF16), v((5120, t), BF16), v((t, 5120), BF16), v((H, 1, t), F32),
             v((2, 1280, 256), BF16), v((2, 1280, 512), BF16), v((2, 5120, 256), BF16), v((4, 320, 1280), BF16),
-            v((t, 512), F32),
+            v((t, 512), F32), v((3,) + part.shape, BF16), v(lengths.shape, F32),
             pltpu.SemaphoreType.DMA, pltpu.SemaphoreType.DMA((2,)), pltpu.SemaphoreType.DMA,
-            pltpu.SemaphoreType.DMA, pltpu.SemaphoreType.DMA, pltpu.SemaphoreType.DMA((6 * layers * 24 + layers,)),
+            pltpu.SemaphoreType.DMA, pltpu.SemaphoreType.DMA, pltpu.SemaphoreType.DMA,
+            pltpu.SemaphoreType.DMA((4,)), pltpu.SemaphoreType.DMA((4,)), pltpu.SemaphoreType.DMA,
+            pltpu.SemaphoreType.DMA((6 * layers * 24 + 14 * layers + 8,)),
         ],
         compiler_params=pltpu.CompilerParams(collective_id=1, has_side_effects=True, vmem_limit_bytes=63 << 20),
         name="forward_all",
-    )(tokens, attn, up, down, vectors, masks)
+    )(tokens, cotangent, *shards, part, lengths)
 
 
 def add(*parts):
@@ -838,7 +942,17 @@
 
 
 ITEMS_A_LAYER = 12
-RING, XRING = 8, 4
+RING, XRING = 10, 4
+ORDERS = ("azb", "baz", "abz", "bza", "azb", "baz", "abz", "bza", "azb", "baz", "abz", "bza")
+PLAN = (
+    -1, -1, -1, -1, -1, 0, 1, -1, 2, 3, -1, 0, 1, -1, -1, 4, 5, 2, 3, -1, -1, -1, 6, 7, 4, 5, 0, 1, -1, 2, 6,
+    3, -1, 4, -1, 8, 7, 0, 1, 2, -1, 5, 3, 4, 0, 1, 2, -1, -1, 6, 7, 0, 1, 2, -1, -1, 9, 10, 8, 5, 3, 4, -1,
+    -2, 3, 4, 9, 5, 11, 5, -1, 6, 7, -1, 10, -1, 12, 11, 8, 9, 13, 14, 10, -1, -2, 11, 15, 12, 13, 6, 7, 8, 6,
+    7, 9, -1, -1, 16, 14, 15, 10, -1, -1, -2, -3, 17, -1, 18, 12, 13, 11, 8, 9, -1, -3, 16, 8, 9, -1, -3, 19,
+    20, 14, 15, 10, -1, -2, -3, 17, 18, 12, 10, -1, -3, 16, 13, 14, 11, -1, 19, 15, 16, 12, 13, 14, 11, -1,
+    12, -1, -2, 13, 14, -1, -4, 20, 17, 21, 22, 15, 16, 15, -4, 16, 18, 19, 21, 23, 20, 17, 21, -4, 17, 17,
+    22, 18, 19, 20, 21, 18, -4, 19, 23, 20, 21, 18, 19, 20, 21, 22, 23, 22, 23, 22, 23, 22, -4, 23
+)
 
 
 def streams(count, copies, body):
@@ -872,17 +986,19 @@
 
 
 def backward_kernel(layers, *refs):
-    (cotangent, attn_full, up_full, down_full, normed_t, qkv, far, lse_all, context_t, middles, hidden_t, slopes,
-     active_t, states, vectors, masks,
-     grad_out, down_out, up_out, out_out, qkv_out, sums,
-     active_far, hidden_far, context_far, normed_far, grad_f_far, grad_pre_far, grad_o_far, grad_far, grad_kv_far,
+    (cotangent, final, attn_full, up_full, down_full, normed_t, qkv, far, lse_all, context_t, middles, hidden_t, slopes,
+     active_t, states, active_far, hidden_far, context_far, normed_far, vectors, masks,
+     output, grad_out, down_out, up_out, out_out, qkv_out, sums,
+     grad_f_far, grad_pre_far, grad_o_far, grad_far, grad_kv_far,
      g, low, gp, gs, gh, rows_in, big, dfar, heads_in, far_in, lse, wide_w, slope_in, left_in,
-     xs, got1s, got2s, got3s, finals,
-     local, lsem, swapped, item_sent, item_local, sent, arrived) = refs
+     xs, got1s, got2s, got3s, finals, sums_held, sums_in,
+     local, lsem, swapped, swapped_half, item_sent, item_local, sums_sent, moved, stayed,
+     sent, arrived) = refs
     a, b, core, z = place()
     to_z = [device(a, b, core, lax.rem(z + s, 4)) for s in range(4)]
     to_a, to_b, to_core = device(1 - a, b, core, z), device(a, 1 - b, core, z), device(a, b, 1 - core, z)
-    greet(to_z[1:] + [to_a, to_b, to_core])
+    stays, to, source = regrouping()
+    greet(to_z[1:] + [to_a, to_b, to_core], (stays, to, source, False))
     net = Net(sent, arrived)
     scale = float(80) ** (-0.5)
     side = {"a": (a, to_a), "b": (b, to_b)}
@@ -944,33 +1060,23 @@
             copy.wait_recv()
         yield
 
-    programs, stage, age = [], [], []
+    programs, stage = [], []
 
     def advance(number):
         next(programs[number])
         stage[number] += 1
 
-    def round_(lead=1):
-        for number in range(len(programs)):
-            age[number] += 1
-            if stage[number] < 7 and (stage[number] > 1 or age[number] >= lead):
-                advance(number)
-
-    def room(extra):
-        while any(stage[i] < 2 for i in range(max(0, len(programs) + extra - XRING))):
-            round_()
-        while any(stage[i] < 5 for i in range(max(0, len(programs) + extra - RING))):
-            round_()
-
     def send_item(order, spot):
         number = len(programs)
+        assert all(s > 4 for s in stage[: max(0, number + 1 - RING)])
         programs.append(program(number, order, spot))
         stage.append(0)
-        age.append(0)
         advance(number)
 
     def weight_gradient(height, own, far_, parts):
         base = len(programs)
+        count = sum(len(part[3]) for part in parts)
+        assert all(s > 1 for s in stage[: max(0, base + count - XRING)])
 
         def copies(i, slot):
             return [
@@ -1021,26 +1127,65 @@
             g[at, :] = out
             sums[layer, pl.ds(gain_at, 1), :] += jnp.sum(grad * unit, axis=0, keepdims=True)
             sums[layer, pl.ds(gain_at + 1, 1), :] += jnp.sum(grad, axis=0, keepdims=True)
+            small = out.astype(BF16)
+            if lowered or layer == 0:
+                low[0, at, :] = small
             if lowered:
-                small = out.astype(BF16)
-                low[0, at, :] = small
                 sums[layer, pl.ds(4, 1), :] += jnp.sum(small.astype(F32), axis=0, keepdims=True)
 
         streams(8, copies, body)
 
-    swaps = {}
-    for layer in reversed(range(layers)):
-        swaps[layer] = [
-            net.push(active_t.at[layer, :, 1 - core], active_far.at[layer], to_core),
-            net.push(hidden_t.at[layer], hidden_far.at[layer], to_core),
-            net.push(context_t.at[layer], context_far.at[layer], to_core),
-            net.push(normed_t.at[layer], normed_far.at[layer], to_core),
+    block = cotangent.shape[1]
+
+    def give_back(values, target, first):
+        return [
+            Swap(net, values.at[pl.ds(step * block, block), :], target.at[lax.rem(z, 2)], to[step], None if step else stays,
+                 moved.at[first + step], stayed.at[first]).start()
+            for step in range(2)
         ]
-    fetch((cotangent, g))
+
+    held = gs.at[:, pl.ds(0, 1280)]
+    fetch((final, held))
+    returned = give_back(held, output, 0)
+    fetch(*[(cotangent.at[step], low.at[0, pl.ds(step * block, block), :]) for step in range(2)])
+
+    @pl.loop(0, 8)
+    def _(i):
+        at = tile(i, 64)
+        g[at, :] = jnp.where(masks[0, at, :] == 0.0, low[0, at, :].astype(F32), 0.0)
+
     sums[...] = jnp.zeros_like(sums)
 
-    for layer in reversed(range(layers)):
+    def sum_program(which, layer, first, size):
+        rows = pl.ds(first, size)
+        steps = [[to_core], [to_b], [to_a], to_z[1:]]
+        sums_held[layer, 0, rows, :] = sums[layer, rows, :]
+        place_in = 0
+        for number, targets in enumerate(steps):
+            copies = [
+                net.push(sums_held.at[layer, number, rows], sums_in.at[layer, place_in + i, rows], target,
+                         sums_sent.at[which, number])
+                for i, target in enumerate(targets)
+            ]
+            yield
+            for copy in copies:
+                copy.wait()
+            all_ = sums_held[layer, number, rows, :]
+            for i in range(len(targets)):
+                all_ = all_ + sums_in[layer, place_in + i, rows, :]
+            place_in += len(targets)
+            if number < 3:
+                sums_held[layer, number + 1, rows, :] = all_
+            else:
+                sums[layer, rows, :] = all_
+        yield
+
+    def work(layer):
         vec = vectors.at[layer]
+        first_item = ITEMS_A_LAYER * (layers - 1 - layer)
+
+        def order_of(item):
+            return ORDERS[item]
 
         @pl.loop(0, 8)
         def _(i):
@@ -1050,10 +1195,9 @@
             sums[layer, pl.ds(7, 1), :] += jnp.sum(small.astype(F32), axis=0, keepdims=True)
 
         swap = net.push(low.at[0], grad_f_far.at[layer], to_core, swapped)
+        yield
         swap.wait()
         fetch((grad_f_far.at[layer], low.at[1]))
-        for copy in swaps[layer]:
-            copy.wait_recv()
 
         def down_spot(half, column):
             def spot(pc, pa, pb):
@@ -1062,26 +1206,30 @@
             return spot
 
         for column in range(2):
-            room(2)
+            orders = [order_of(2 * column), order_of(2 * column + 1)]
             weight_gradient(
                 640, lambda i: active_t.at[layer, i, core], lambda i: active_far.at[layer, i],
                 [(lambda column=column: low[0, :, column * 640 : column * 640 + 640],
                   lambda column=column: low[1, :, column * 640 : column * 640 + 640], 1.0,
-                  [(0, "azb", 0), (1, "bza", 80)])],
+                  [(0, orders[0], 0), (1, orders[1], 80)])],
             )
-            send_item("azb", down_spot(0, column))
-            send_item("bza", down_spot(1, column))
-            if column == 0:
-                round_()
+            send_item(orders[0], down_spot(0, column))
+            send_item(orders[1], down_spot(1, column))
+            yield
+
+        def unit_of(i):
+            return lax.rem(i + 5 * (1 - core), 10)
 
         def copies_down(i, slot):
+            at = tile(unit_of(i), 512)
             return [
-                pltpu.make_async_copy(down_full.at[layer, tile(i, 512), :], wide_w.at[slot], lsem.at[slot]),
-                pltpu.make_async_copy(slopes.at[layer, :, tile(i, 512)], slope_in.at[slot], lsem.at[slot]),
+                pltpu.make_async_copy(down_full.at[layer, at, :], wide_w.at[slot], lsem.at[slot]),
+                pltpu.make_async_copy(slopes.at[layer, :, at], slope_in.at[slot], lsem.at[slot]),
             ]
 
         def body_down(i, slot):
-            at = tile(i, 512)
+            unit = unit_of(i)
+            at = tile(unit, 512)
             gh[:, :512] = dot(low[0], wide_w[slot], NT)
 
             @pl.loop(0, 8)
@@ -1089,13 +1237,17 @@
                 rows = tile(j, 64)
                 small = (gh[rows, :512] * slope_in[slot, rows, :].astype(F32)).astype(BF16)
                 gp[rows, at] = small
-                sums[layer, pl.ds(8 + i, 1), :512] += jnp.sum(small.astype(F32), axis=0, keepdims=True)
-
-        streams(10, copies_down, body_down)
+                sums[layer, pl.ds(8 + unit, 1), :512] += jnp.sum(small.astype(F32), axis=0, keepdims=True)
+
+        streams(5, copies_down, body_down)
         swap = net.push(gp.at[:, pl.ds(pl.multiple_of((1 - core) * 2560, 128), 2560)], grad_pre_far.at[layer], to_core,
                         swapped)
-        round_()
+        yield
+        streams(5, lambda i, slot: copies_down(i + 5, slot), lambda i, slot: body_down(i + 5, slot))
+        yield
         swap.wait()
+        while layer == layers - 1 and returned:
+            returned.pop().wait()
         fetch((grad_pre_far.at[layer], gs))
 
         def up_spot(unit):
@@ -1108,17 +1260,16 @@
             return values.at[layer, pl.ds(pl.multiple_of(i * 320, 16), 320), :]
 
         for pair in range(2):
-            room(2)
+            orders = [order_of(4 + 2 * pair), order_of(5 + 2 * pair)]
             weight_gradient(
                 320, lambda i: rows_of(hidden_t, i), lambda i: rows_of(hidden_far, i),
                 [(lambda unit=unit: gp[:, pl.ds(pl.multiple_of(core * 2560 + unit * 640, 128), 640)],
                   lambda unit=unit: gs[:, unit * 640 : unit * 640 + 640], 1.0,
-                  [(unit % 2, ("azb", "bza")[unit % 2], 0)]) for unit in (2 * pair, 2 * pair + 1)],
+                  [(unit % 2, orders[unit % 2], 0)]) for unit in (2 * pair, 2 * pair + 1)],
             )
-            send_item("azb", up_spot(2 * pair))
-            send_item("bza", up_spot(2 * pair + 1))
-            if pair == 0:
-                round_()
+            send_item(orders[0], up_spot(2 * pair))
+            send_item(orders[1], up_spot(2 * pair + 1))
+            yield
 
         def copies_up(i, slot):
             return [
@@ -1136,10 +1287,11 @@
             gh[:, tile(i, 256)] = total_
 
         streams(5, copies_up, body_up)
-        round_()
+        yield
         norm_back(middles.at[layer], vec[5:6, :], 5, layer, True)
         swap = net.push(low.at[0, :, pl.ds(pl.multiple_of((1 - core) * 640, 128), 640)], grad_o_far.at[layer], to_core,
                         swapped)
+        yield
 
         def copies_out(i, slot):
             return [pltpu.make_async_copy(attn_full.at[layer, 3, tile(i, 256), :], wide_w.at[slot, pl.ds(0, 256), :],
@@ -1159,14 +1311,13 @@
                                 pl.ds(pl.multiple_of(pc * 640, 128), 640)]
             return spot
 
-        room(1)
         weight_gradient(
             320, lambda i: rows_of(context_t, i), lambda i: rows_of(context_far, i),
             [(lambda: low[0, :, pl.ds(pl.multiple_of(core * 640, 128), 640)], lambda: low[1, :, :640], 1.0,
-              [(0, "abz", 0)])],
+              [(0, order_of(8), 0)])],
         )
-        send_item("abz", small_spot(out_out.at[layer]))
-        round_()
+        send_item(order_of(8), small_spot(out_out.at[layer]))
+        yield
 
         def copies_head(h, slot):
             at = pl.ds(pl.multiple_of(h * 80, 16), 80)
@@ -1197,11 +1348,16 @@
                 target[...] = dot(query, ds, NT).astype(BF16)
             big[at, :] = total_.astype(BF16)
 
-        for part in range(2):
-            streams(8, lambda i, slot: copies_head(i + 8 * part, slot), lambda i, slot: body_head(i + 8 * part, slot))
-            round_()
-        swap = net.push(dfar, grad_kv_far.at[layer], to_core, swapped)
-        swap.wait()
+        swap = []
+        for part in range(4):
+            streams(4, lambda i, slot: copies_head(i + 4 * part, slot), lambda i, slot: body_head(i + 4 * part, slot))
+            if part % 2 == 1:
+                rows = pl.ds(320 * (2 * (part // 2)), 640)
+                swap.append(net.push(dfar.at[:, rows, :], grad_kv_far.at[layer, :, rows, :], to_core,
+                                     swapped_half.at[part // 2]))
+            yield
+        for copy in swap:
+            copy.wait()
 
         def copies_far(i, slot):
             return [pltpu.make_async_copy(grad_kv_far.at[layer, :, tile(i, 128), :], far_in.at[slot], lsem.at[slot])]
@@ -1210,13 +1366,13 @@
             at = tile(i, 128)
             query = big[at, :].T
             gp[:, at] = query
-            sums[layer, 2:3, at] = jnp.sum(query.astype(F32), axis=0, keepdims=True) * scale
+            sums[layer, 20:21, at] = jnp.sum(query.astype(F32), axis=0, keepdims=True) * scale
             for which in range(2):
                 rows = pl.ds(pl.multiple_of(1280 + which * 1280 + i * 128, 128), 128)
                 both = (big[rows, :].astype(F32) + far_in[slot, which].astype(F32)).astype(BF16).T
                 gp[:, pl.ds(pl.multiple_of(1280 + which * 1280 + i * 128, 128), 128)] = both
                 if which == 1:
-                    sums[layer, 3:4, at] = jnp.sum(both.astype(F32), axis=0, keepdims=True)
+                    sums[layer, 21:22, at] = jnp.sum(both.astype(F32), axis=0, keepdims=True)
 
         streams(10, copies_far, body_far)
         swap = [
@@ -1224,52 +1380,61 @@
                      to_core, swapped)
             for t in range(3)
         ]
+        yield
+
+        def copies_back(i, slot):
+            return [pltpu.make_async_copy(attn_full.at[layer, i // 5, tile(i % 5, 256), :],
+                                          wide_w.at[slot, pl.ds(0, 256), :], lsem.at[slot])]
+
+        def body_back(i, slot):
+            at = tile(i % 5, 256)
+            out = dot(gp[:, pl.ds(pl.multiple_of((i // 5) * 1280, 128), 1280)], wide_w[slot, :256, :], NT)
+
+            @pl.when(i < 5)
+            def _():
+                gh[:, at] = out * scale
+
+            @pl.when(i >= 5)
+            def _():
+                gh[:, at] += out
+
+        streams(5, copies_back, body_back)
         for copy in swap:
             copy.wait()
         fetch(*[(grad_far.at[layer, t], gs.at[:, pl.ds(t * 640, 640)]) for t in range(3)])
         for group in ((0, 1), (2,)):
-            room(len(group))
             weight_gradient(
                 320, lambda i: rows_of(normed_t, i), lambda i: rows_of(normed_far, i),
                 [(lambda t=t: gp[:, pl.ds(pl.multiple_of(t * 1280 + core * 640, 128), 640)],
                   lambda t=t: gs[:, t * 640 : t * 640 + 640], scale if t == 0 else 1.0,
-                  [(t % 2, ("baz", "abz")[t % 2], 0)]) for t in group],
+                  [(t % 2, order_of(9 + t), 0)]) for t in group],
             )
             for t in group:
-                send_item(("baz", "abz")[t % 2], small_spot(qkv_out.at[layer, t]))
-            if len(group) == 2:
-                round_()
-
-        def copies_back(i, slot):
-            return [pltpu.make_async_copy(attn_full.at[layer, i // 5, tile(i % 5, 256), :],
-                                          wide_w.at[slot, pl.ds(0, 256), :], lsem.at[slot])]
-
-        def body_back(i, slot):
-            at = tile(i % 5, 256)
-            out = dot(gp[:, pl.ds(pl.multiple_of((i // 5) * 1280, 128), 1280)], wide_w[slot, :256, :], NT)
-
-            @pl.when(i < 5)
-            def _():
-                gh[:, at] = out * scale
-
-            @pl.when(i >= 5)
-            def _():
-                gh[:, at] += out
-
-        streams(15, copies_back, body_back)
-        round_()
-        norm_back(states.at[layer], vec[0:1, :], 0, layer, False)
-        if layer > 0:
-            round_()
-    store = pltpu.make_async_copy(g, grad_out, local)
-    store.start()
-    while any(s < 7 for s in stage):
-        round_()
-    store.wait()
+                send_item(order_of(9 + t), small_spot(qkv_out.at[layer, t]))
+            yield
+        streams(10, lambda i, slot: copies_back(i + 5, slot), lambda i, slot: body_back(i + 5, slot))
+        yield
+        norm_back(states.at[layer], vec[0:1, :], 18, layer, False)
+        if layer == 0:
+            returned.extend(give_back(low.at[0], grad_out, 2))
+        yield
+
+    sum_programs = [sum_program(0, 1, 0, 24), sum_program(1, 0, 0, 16), sum_program(2, 0, 16, 8)]
+    segments = itertools.chain.from_iterable(work(layer) for layer in reversed(range(layers)))
+    for action in PLAN:
+        if action == -1:
+            next(segments)
+        elif action < 0:
+            next(sum_programs[-2 - action])
+        else:
+            advance(action)
+    for copy in returned:
+        copy.wait()
+    assert next(segments, None) is None and all(s == 7 for s in stage)
     net.drain()
 
 
-def backward_all(cotangent, weights, kept, vectors, masks):
+def backward_all(cotangent, final, weights, kept, vectors, masks):
     any_ = pl.BlockSpec(memory_space=pl.ANY)
     vmem = pl.BlockSpec(memory_space=pltpu.VMEM)
     layers = vectors.shape[0]
@@ -1279,71 +1444,34 @@
         return jax.ShapeDtypeStruct((layers,) + shape, dtype)
 
     out_shape = (
-        jax.ShapeDtypeStruct((t, 1280), F32), hbm((1280, 1280)), hbm((320, 5120)), hbm((320, 1280)), hbm((3, 320, 1280)),
+        jax.ShapeDtypeStruct(cotangent.shape, BF16), jax.ShapeDtypeStruct(cotangent.shape, BF16),
+        hbm((1280, 1280)), hbm((320, 5120)), hbm((320, 1280)), hbm((3, 320, 1280)),
         hbm((24, 1280), F32),
-        hbm((4, 640, t)), hbm((1280, t)), hbm((1280, t)), hbm((1280, t)), hbm((t, 1280)), hbm((t, 2560)), hbm((t, 640)),
-        hbm((3, t, 640)), hbm((2, 1280, t)),
+        hbm((t, 1280)), hbm((t, 2560)), hbm((t, 640)), hbm((3, t, 640)), hbm((2, 1280, t)),
     )
     v = pltpu.VMEM
     items = ITEMS_A_LAYER * layers
     return pl.pallas_call(
         functools.partial(backward_kernel, layers),
         out_shape=out_shape,
-        in_specs=[any_] * 14 + [vmem] * 2,
-        out_specs=(any_,) * 5 + (vmem,) + (any_,) * 9,
+        in_specs=[any_] * 19 + [vmem] * 2,
+        out_specs=(any_,) * 6 + (vmem,) + (any_,) * 5,
         scratch_shapes=[
             v((t, 1280), F32), v((2, t, 1280), BF16), v((t, 5120), BF16), v((t, 2560), BF16), v((t, 1280), F32),
             v((2, 64, 1280), F32), v((5120, t), BF16), v((2, 1280, t), BF16), v((2, 5, 80, t), BF16), v((2, 2, 128, t), BF16),
             v((H, 1, t), F32), v((2, 512, 1280), BF16), v((2, t, 512), BF16), v((2, 2, 640, t), BF16),
             v((XRING, 2, 4, 2, 80, 640), BF16), v((RING, 4, 2, 80, 640), BF16), v((RING, 6, 80, 640), BF16),
             v((RING, 3, 80, 640), BF16), v((RING, 80, 640), BF16),
+            v((layers, 4, 24, 1280), F32), v((layers, 6, 24, 1280), F32),
             pltpu.SemaphoreType.DMA, pltpu.SemaphoreType.DMA((2,)), pltpu.SemaphoreType.DMA,
-            pltpu.SemaphoreType.DMA((RING, 4)), pltpu.SemaphoreType.DMA((RING,)), pltpu.SemaphoreType.DMA,
-            pltpu.SemaphoreType.DMA((items * 12 + 12 * layers,)),
+            pltpu.SemaphoreType.DMA((2,)),
+            pltpu.SemaphoreType.DMA((RING, 4)), pltpu.SemaphoreType.DMA((RING,)), pltpu.SemaphoreType.DMA((3, 4)),
+            pltpu.SemaphoreType.DMA((4,)), pltpu.SemaphoreType.DMA((4,)), pltpu.SemaphoreType.DMA,
+            pltpu.SemaphoreType.DMA((items * 12 + 16 * layers + 8,)),
         ],
         compiler_params=pltpu.CompilerParams(collective_id=2, has_side_effects=True, vmem_limit_bytes=63 << 20),
         name="backward_all",
-    )(cotangent, *weights, *kept, vectors, masks)
-
-
-def total_kernel(values, out, held, got, sent, arrived):
-    a, b, core, z = place()
-    to_z = [device(a, b, core, lax.rem(z + s, 4)) for s in (1, 2, 3)]
-    steps = [[device(a, b, 1 - core, z)], [device(a, 1 - b, core, z)], [device(1 - a, b, core, z)], to_z]
-    greet([target for step in steps for target in step])
-    net = Net(sent, arrived)
-    held[0] = values[...]
-    place_of = 0
-    for number, step in enumerate(steps):
-        first = place_of
-        copies = []
-        for target in step:
-            copies.append(net.push(held.at[number], got.at[place_of], target))
-            place_of += 1
-        sum_ = held[number]
-        for i, copy in enumerate(copies):
-            copy.wait_recv()
-            sum_ = sum_ + got[first + i]
-        if number < 3:
-            held[number + 1] = sum_
-        else:
-            out[...] = sum_
-    net.drain()
-
-
-def total(values):
-    vmem = pl.BlockSpec(memory_space=pltpu.VMEM)
-    return pl.pallas_call(
-        total_kernel,
-        out_shape=jax.ShapeDtypeStruct(values.shape, F32),
-        in_specs=[vmem], out_specs=vmem,
-        scratch_shapes=[
-            pltpu.VMEM((4,) + values.shape, F32), pltpu.VMEM((6,) + values.shape, F32),
-            pltpu.SemaphoreType.DMA, pltpu.SemaphoreType.DMA((6,)),
-        ],
-        compiler_params=pltpu.CompilerParams(collective_id=3, has_side_effects=True),
-        name="total",
-    )(values)
+    )(cotangent, final, *weights, *kept, vectors, masks)
 
 
 def plane_shards(
@@ -1351,73 +1479,26 @@
     value_weight, value_bias, out_weight, out_bias, mlp_gain, mlp_shift, up_weight, up_bias,
     down_weight, down_bias,
 ):
-    a, b, core, z = place()
+    z = lax.axis_index("shard")
     layers = attn_gain.shape[0]
-    block = inputs.shape[1]
-
-    def gather_tokens(values):
-        return jnp.concatenate(
-            [send(pick(values, (z + step) % 2), "in%d" % step) for step in range(2)], axis=0
-        )
-
-    def return_tokens(values):
-        got = [send(values[step * block : (step + 1) * block], "out%d" % step) for step in range(2)]
-        got = jnp.stack(got)
-        return jnp.stack([pick(got, (z + clip) % 2) for clip in range(2)])
-
-    packed = jnp.concatenate(
-        [attn_gain, attn_shift, query_bias, value_bias, out_bias, mlp_gain, mlp_shift, down_bias,
-         up_bias], axis=1,
-    )
-    pieces = jnp.stack([packed] + [send(packed, "z%d" % s) for s in (1, 2, 3)])
-    pieces = jnp.stack([pick(pieces, (z + 4 - from_z) % 4) for from_z in range(4)]).astype(F32)
-    vectors = []
-    for layer in range(layers):
-        row = [pieces[:, layer, i * 320 : (i + 1) * 320].reshape(1280) for i in range(8)]
-        row.append(pieces[:, layer, 2560:].reshape(5120))
-        vectors.append(tuple(row))
-
-    state = gather_tokens(inputs).astype(F32)
-
-    far_lengths = send(lengths, "core")
-    four = jnp.where(core == 0, jnp.concatenate([lengths, far_lengths]),
-                     jnp.concatenate([far_lengths, lengths]))
-    length = pick(four, z)
-
-    def positions(which):
-        return jnp.concatenate(
-            [(2 * which + (z + step) % 2) * block + jnp.arange(block) for step in range(2)]
-        )
-
-    def mask_of(which):
-        return jnp.where(positions(which) < length, 0.0, NEGATIVE).astype(F32)[:, None]
-
-    masks = (mask_of(core), mask_of(1 - core))
-
-    table = jnp.zeros((layers, 24, 1280), F32)
-    for layer in range(layers):
-        rows = jnp.stack(vectors[layer][:8])
-        wide = jnp.pad(vectors[layer][8].reshape(10, 512), ((0, 0), (0, 768)))
-        table = table.at[layer, :18].set(jnp.concatenate([rows, wide]))
-    attn = jnp.stack([query_weight, key_weight, value_weight, out_weight], axis=1)
-    (attn, up, down, normed_t, qkv, far, lse, context_t, middles, hidden_t, slopes, active_t, states) = forward_all(
-        state, attn, up_weight, down_weight, table, jnp.stack(masks)
-    )
-    state = states[layers]
-    output = return_tokens(state.astype(BF16))
-
-    row_mask = (positions(core) < length).astype(F32)
-    grad = gather_tokens(cotangent).astype(F32) * row_mask[:, None]
-    lse_mask = jnp.stack(masks)
-    results = backward_all(
-        grad, (attn, up, down),
-        (normed_t, qkv, far, lse, context_t, middles, hidden_t, slopes, active_t.reshape(layers, 4, 2, 640, -1), states),
-        table, lse_mask,
-    )
-    grad, down_grad, up_grad, out_grad, qkv_grad, small = results[:6]
-    input_grad = return_tokens(grad.astype(BF16)).astype(F32)
-    small = jnp.concatenate([small[:, :8].reshape(layers, -1), small[:, 8:18, :512].reshape(layers, -1)], axis=1)
-    sums = total(small.reshape(-1, 128)).reshape(layers, -1)
+    rows = jnp.stack([attn_gain, attn_shift, query_bias, value_bias, out_bias, mlp_gain, mlp_shift, down_bias], axis=1)
+    part = jnp.zeros((layers, 24, 1280), BF16)
+    part = lax.dynamic_update_slice(part, rows, (0, 0, z * 320))
+    wide = lax.dynamic_update_slice(jnp.zeros((layers, 5120), BF16), up_bias, (0, z * 1280)).reshape(layers, 10, 512)
+    part = lax.dynamic_update_slice(part, wide, (0, 8, 0))
+    spread = jnp.broadcast_to(lengths.astype(F32)[:, None, None], (2, 8, 128))
+    results = forward_all(
+        inputs, cotangent, (query_weight, key_weight, value_weight, out_weight, up_weight, down_weight), part, spread
+    )
+    weights, kept = results[:3], list(results[3:17])
+    cotangent, final, table, masks = results[17:]
+    kept[8] = kept[8].reshape(layers, 4, 2, 640, -1)
+    output, grad, down_grad, up_grad, out_grad, qkv_grad, small = backward_all(
+        cotangent, final, weights, kept, table, masks
+    )[:7]
+    input_grad = grad.astype(F32)
+    small_rows = jnp.concatenate([small[:, 18:22], small[:, 4:8]], axis=1)
+    sums = jnp.concatenate([small_rows.reshape(layers, -1), small[:, 8:18, :512].reshape(layers, -1)], axis=1)
     vec = pick(sums[:, :10240].reshape(layers, 8, 4, 320), z, 2)
     up_bias_grad = pick(sums[:, 10240:].reshape(layers, 4, 1280), z, 1)
 

time: 1150 us -> 924 us (0.80)
  Pallas kernels: 1000 us -> 871 us
  waiting for transfers between devices: 36.3 us -> 0 us
  starting transfers between devices: 27.3 us -> 0 us
  other arithmetic: 46.8 us -> 23.7 us
    pallas_call x1, Pallas kernels: 666 us -> 516 us  [backward_all(): pl.pallas_call(functools.partial(backward_kernel, layers), out_shape=out_...]
    pallas_call x1, Pallas kernels: 316 us -> 355 us  [forward_all(): pl.pallas_call(functools.partial(forward_kernel, layers), out_shape=out_s...]
    ppermute x12 -> x0, waiting for transfers between devices: 36.3 us -> none  [send(): return lax.ppermute(values, BOTH, PAIRS[way])]
    ppermute x12 -> x0, starting transfers between devices: 27.3 us -> none  [send(): return lax.ppermute(values, BOTH, PAIRS[way])]
    pallas_call x1 -> x0, Pallas kernels: 22.5 us -> none  [total(): pl.pallas_call(total_kernel, out_shape=jax.ShapeDtypeStruct(values.shape,...]
    another operation x7 -> x0, other arithmetic: 15.2 us -> none
  transfers between devices with their start and end apart: 12 -> 0, of which waited for: 3 -> 0; matrix products, arithmetic and copies ran while one was open for 4% -> 0% of each run, Pallas kernels for 28% -> 0%
where the time goes in v1:
time: 924 us; the launch traced here: 910 us
  Pallas kernels  871 us (94%)
  other arithmetic  23.7 us (3%)
  local copies, waits for them, and re-layouts  13.8 us (1%)
    pallas_call x1, Pallas kernels, backward_all(): pl.pallas_call(functools.partial(backward_kernel, layers), out_shape=out_...  516 us
    pallas_call x1, Pallas kernels, forward_all(): pl.pallas_call(functools.partial(forward_kernel, layers), out_shape=out_s...  355 us

profile of v1, /device:TPU:11, one launch (start us, length us, event | category | flops | bytes accessed | tf_op | source)
XLA Modules:
  0.0 909.6 jit_solution(8538410236171441486)
XLA Ops:
  0.7 0.7 convert_element_type.33
  1.3 0.7 copy.36
  2.0 0.7 copy.37
  2.7 0.7 copy.38
  3.4 0.7 copy.39
  4.1 0.7 copy.40
  4.7 0.7 copy.41
  5.4 0.7 copy.42
  6.1 0.7 copy.43
  6.8 0.1 stack.35
  6.8 0.7 broadcast_in_dim.14.refs_9_
  7.5 0.7 constant_dynamic-update-slice_fusion
  8.3 1.2 dynamic_update_slice.9
  9.4 0.7 dynamic_update_slice.11.refs_8_
  10.1 0.0 copy-start.3
  10.1 0.6 copy-done.3
  10.8 355.3 %forward_all.1 = (bf16[2,4,1280,1280]{3,2,1,0:T(8,128)(2,1)}, bf16[2,1280,5120]{2,1,0:T(8,128)(2,1)}, bf16[2,5120,1280]{2,1,0:T(8,128)(2,1)}, bf16[2,1280,512]{2...) custom-call(bf16[2,256,1280]{2,1,0:T(8,128)(2,1)} %refs_0_.1, ...), custom_call_target="tpu_custom_call" | custom-call | tf_op jit(solution)/shard_map/forward_all/pallas_call | solution.py:916
  366.1 515.5 %backward_all.1 = (bf16[2,256,1280]{2,1,0:T(8,128)(2,1)}, bf16[2,256,1280]{2,1,0:T(8,128)(2,1)}, bf16[2,1280,1280]{2,1,0:T(8,128)(2,1)}, bf16[2,320,5120]{2,1,0:...) custom-call(bf16[2,256,1280]{2,1,0:T(8,128)(2,1)} %get-tuple-element, ...), custom_call_target="tpu_custom_call" | custom-call | tf_op jit(solution)/shard_map/backward_all/pallas_call | solution.py:1454
  881.7 0.0 copy-start.1
  881.7 1.0 slice.54
  882.6 0.9 fusion
  883.6 0.6 copy.49
  884.3 0.1 reshape_reshape.6
  884.5 0.6 slice_bitcast_fusion
  885.1 0.0 copy-start
  885.1 3.1 convert_element_type.34
  888.2 0.0 copy-done.1
  888.2 0.0 slice-start.2
  888.2 2.0 convert_element_type.41
  890.2 0.0 copy-done
  890.2 0.0 slice-start.3
  890.2 0.0 slice-start
  890.2 5.1 bitcast_convert_fusion
  895.3 0.0 slice-done.2
  895.3 0.0 slice-done.3
  895.3 0.0 slice-start.1
  895.3 6.8 convert_element_type.42
  902.1 0.0 slice-done
  902.1 0.0 slice-done.1
  902.1 0.0 copy-start.2
  902.1 6.0 convert_element_type.43
  908.1 0.0 copy-done.2
  908.1 1.1 copy.54
  (10 shorter events, 0.1 us)
Async XLA Ops:
  10.1 0.7 copy-start.3
  881.7 6.6 copy-start.1
  885.1 5.1 copy-start
  888.2 7.1 slice-start.2
  890.2 5.2 slice-start.3
  890.2 11.9 %slice-start = ((s8[6553600]{0:T(1024)(128)(4,1)}), s8[4194304]{0:T(1024)(128)(4,1)S(1)}, s32[]{:S(2)}) async-start(s8[6553600]{0:T(1024)(128)(4,1)} %bitcast.41), calls=%async_computation | async-start | bytes 8388608
  895.3 6.8 slice-start.1
  902.1 6.0 copy-start.2

commit v2 on v1

--- a/solution.py
+++ b/solution.py
@@ -947,11 +947,11 @@
 PLAN = (
     -1, -1, -1, -1, -1, 0, 1, -1, 2, 3, -1, 0, 1, -1, -1, 4, 5, 2, 3, -1, -1, -1, 6, 7, 4, 5, 0, 1, -1, 2, 6,
     3, -1, 4, -1, 8, 7, 0, 1, 2, -1, 5, 3, 4, 0, 1, 2, -1, -1, 6, 7, 0, 1, 2, -1, -1, 9, 10, 8, 5, 3, 4, -1,
-    -2, 3, 4, 9, 5, 11, 5, -1, 6, 7, -1, 10, -1, 12, 11, 8, 9, 13, 14, 10, -1, -2, 11, 15, 12, 13, 6, 7, 8, 6,
-    7, 9, -1, -1, 16, 14, 15, 10, -1, -1, -2, -3, 17, -1, 18, 12, 13, 11, 8, 9, -1, -3, 16, 8, 9, -1, -3, 19,
-    20, 14, 15, 10, -1, -2, -3, 17, 18, 12, 10, -1, -3, 16, 13, 14, 11, -1, 19, 15, 16, 12, 13, 14, 11, -1,
-    12, -1, -2, 13, 14, -1, -4, 20, 17, 21, 22, 15, 16, 15, -4, 16, 18, 19, 21, 23, 20, 17, 21, -4, 17, 17,
-    22, 18, 19, 20, 21, 18, -4, 19, 23, 20, 21, 18, 19, 20, 21, 22, 23, 22, 23, 22, 23, 22, -4, 23
+    3, 4, 9, 5, 11, 5, -1, 6, 7, -1, 10, -1, 12, 11, 8, 9, 13, 14, 10, -1, 11, 15, 12, 13, 6, 7, 8, 6, 7, 9,
+    -1, -1, 16, 14, 15, 10, -1, -1, 17, -1, 18, 12, 13, 11, 8, 9, -1, 16, 8, 9, -1, 19, 20, 14, 15, 10, -1,
+    17, 18, 12, 10, -1, 16, 13, 14, 11, -1, 19, 15, 16, 12, 13, 14, 11, -1, 12, -1, 13, 14, -1, -4, -3, -2,
+    20, 17, 21, 22, 15, 16, 15, -4, -3, -2, 16, 18, 19, 21, 23, 20, 17, 21, -4, -3, -2, 17, 17, 22, 18, 19,
+    20, 21, 18, -4, -3, -2, 19, 23, 20, 21, 18, 19, 20, 21, 22, 23, 22, 23, 22, 23, 22, -4, -3, -2, 23
 )
 
 

time: 924 us -> 879 us (0.951)
  Pallas kernels: 871 us -> 826 us
    pallas_call x1, Pallas kernels: 516 us -> 470 us  [backward_all(): pl.pallas_call(functools.partial(backward_kernel, layers), out_shape=out_...]
where the time goes in v2:
time: 879 us; the launch traced here: 864 us
  Pallas kernels  826 us (94%)
  other arithmetic  23.7 us (3%)
  local copies, waits for them, and re-layouts  13.8 us (2%)
    pallas_call x1, Pallas kernels, backward_all(): pl.pallas_call(functools.partial(backward_kernel, layers), out_shape=out_...  470 us
    pallas_call x1, Pallas kernels, forward_all(): pl.pallas_call(functools.partial(forward_kernel, layers), out_shape=out_s...  355 us

profile of v2, /device:TPU:11, one launch (start us, length us, event | category | flops | bytes accessed | tf_op | source)
XLA Modules:
  0.0 864.4 jit_solution(18272286522784098466)
XLA Ops:
  0.7 0.7 convert_element_type.33
  1.3 0.7 copy.36
  2.0 0.7 copy.37
  2.7 0.7 copy.38
  3.4 0.7 copy.39
  4.1 0.7 copy.40
  4.7 0.7 copy.41
  5.4 0.7 copy.42
  6.1 0.7 copy.43
  6.8 0.1 stack.35
  6.8 0.7 broadcast_in_dim.14.refs_9_
  7.5 0.7 constant_dynamic-update-slice_fusion
  8.3 1.2 dynamic_update_slice.9
  9.4 0.7 dynamic_update_slice.11.refs_8_
  10.1 0.0 copy-start.3
  10.1 0.6 copy-done.3
  10.8 355.3 %forward_all.1 = (bf16[2,4,1280,1280]{3,2,1,0:T(8,128)(2,1)}, bf16[2,1280,5120]{2,1,0:T(8,128)(2,1)}, bf16[2,5120,1280]{2,1,0:T(8,128)(2,1)}, bf16[2,1280,512]{2...) custom-call(bf16[2,256,1280]{2,1,0:T(8,128)(2,1)} %refs_0_.1, ...), custom_call_target="tpu_custom_call" | custom-call | tf_op jit(solution)/shard_map/forward_all/pallas_call | solution.py:916
  366.1 470.4 %backward_all.1 = (bf16[2,256,1280]{2,1,0:T(8,128)(2,1)}, bf16[2,256,1280]{2,1,0:T(8,128)(2,1)}, bf16[2,1280,1280]{2,1,0:T(8,128)(2,1)}, bf16[2,320,5120]{2,1,0:...) custom-call(bf16[2,256,1280]{2,1,0:T(8,128)(2,1)} %get-tuple-element, ...), custom_call_target="tpu_custom_call" | custom-call | tf_op jit(solution)/shard_map/backward_all/pallas_call | solution.py:1454
  836.5 0.0 copy-start.1
  836.5 1.0 slice.54
  837.5 0.9 fusion
  838.5 0.6 copy.49
  839.1 0.1 reshape_reshape.6
  839.3 0.6 slice_bitcast_fusion
  839.9 0.0 copy-start
  839.9 3.1 convert_element_type.34
  843.0 0.0 copy-done.1
  843.0 0.0 slice-start.2
  843.0 2.0 convert_element_type.41
  845.0 0.0 copy-done
  845.0 0.0 slice-start.3
  845.0 0.0 slice-start
  845.0 5.1 bitcast_convert_fusion
  850.1 0.0 slice-done.2
  850.2 0.0 slice-done.3
  850.2 0.0 slice-start.1
  850.2 6.8 convert_element_type.42
  856.9 0.0 slice-done
  856.9 0.0 slice-done.1
  856.9 0.0 copy-start.2
  856.9 6.0 convert_element_type.43
  862.9 0.0 copy-done.2
  862.9 1.1 copy.54
  (10 shorter events, 0.1 us)
Async XLA Ops:
  10.1 0.7 copy-start.3
  836.5 6.6 copy-start.1
  839.9 5.1 copy-start
  843.0 7.1 slice-start.2
  845.0 5.2 slice-start.3
  845.0 11.9 %slice-start = ((s8[6553600]{0:T(1024)(128)(4,1)}), s8[4194304]{0:T(1024)(128)(4,1)S(1)}, s32[]{:S(2)}) async-start(s8[6553600]{0:T(1024)(128)(4,1)} %bitcast.41), calls=%async_computation | async-start | bytes 8388608
  850.2 6.8 slice-start.1
  856.9 6.0 copy-start.2

commit v3 on v2

--- a/solution.py
+++ b/solution.py
@@ -444,7 +444,7 @@
 class Net:
     def __init__(self, sent, arrived):
         self.sent, self.arrived = sent, arrived
-        self.copies, self.count = [], 0
+        self.copies, self.some, self.count = [], [], 0
     def push(self, source, target_ref, target, sent=None):
         copy = pltpu.make_async_remote_copy(
             src_ref=source, dst_ref=target_ref, send_sem=self.sent if sent is None else sent,
@@ -455,9 +455,21 @@
             self.copies.append(copy)
         return copy
 
+    def push_if(self, wanted, source, target_ref, target, at=None):
+        copy = pltpu.make_async_remote_copy(
+            src_ref=source, dst_ref=target_ref, send_sem=self.sent,
+            recv_sem=self.arrived.at[self.count if at is None else at], device_id=target, device_id_type=MESH)
+        pl.when(wanted)(lambda: copy.start())
+        if at is None:
+            self.count += 1
+        self.some.append((wanted, copy))
+        return copy
+
     def drain(self):
         for copy in self.copies:
             copy.wait_send()
+        for wanted, copy in self.some:
+            pl.when(wanted)(lambda copy=copy: copy.wait_send())
 
 def greet(targets, regroup=None):
     barrier = pltpu.get_barrier_semaphore()
@@ -580,16 +592,35 @@
         which, at = gather_regions(index % 6, zs, pa * 2 + pb, core)
         return whose[which].at[index // 6].at[at]
 
+    starts = [None, z != 3, None, z != 0]
+    inner = jnp.logical_and(z > 0, z < 3)
+    to_end = device(a, b, core, jnp.where(z == 2, 3, 0))
+    first_slot = {}
+
     def start(index):
-        if index % 6 > 1:
-            return [[net.push(refs_at(index, 0, a, b, shards), refs_at(index, z, a, b, outs), to_z[s])] for s in (1, 2, 3)]
-        here, there = [
-            pl.ds(pl.multiple_of(zs * 320 + ((a * 2 + b) * 2 + core) * 40, 8), 40) for zs in (0, z)]
+        first_slot[index] = net.count
+        layer, within = index // 6, index % 6
+        pieces = [(refs_at(index, 0, a, b, shards), refs_at(index, z, a, b, outs))] if within > 1 else []
+        if within < 2:
+            here, there = [
+                pl.ds(pl.multiple_of(zs * 320 + ((a * 2 + b) * 2 + core) * 40, 8), 40) for zs in (0, z)]
+            pieces = [(shards[0][i].at[layer, here, :], outs[0].at[layer, i, there, :])
+                      for i in (2 * within, 2 * within + 1)]
         return [
-            [net.push(shards[0][i].at[index // 6, here, :], outs[0].at[index // 6, i, there, :], to_z[s])
-             for i in (2 * (index % 6), 2 * (index % 6) + 1)]
+            [net.push(x, y, to_z[s]) if starts[s] is None else net.push_if(starts[s], x, y, to_z[s]) for x, y in pieces]
             for s in (1, 2, 3)
         ]
+
+    def pass_on(index):
+        within = index % 6
+        if within > 1:
+            refs = [refs_at(index, behind[2], a, b, outs)]
+        else:
+            rows = pl.ds(pl.multiple_of(behind[2] * 320 + ((a * 2 + b) * 2 + core) * 40, 8), 40)
+            refs = [outs[0].at[index // 6, i, rows, :] for i in (2 * within, 2 * within + 1)]
+        for i, ref in enumerate(refs):
+            slot = first_slot[index] + i
+            net.push_if(inner, ref, ref, to_end, jnp.where(z == 2, slot + 2 * len(refs), slot))
 
     def on(index, s, pa, pb, target):
         ref = refs_at(index, behind[s], pa, pb, outs)
@@ -597,6 +628,13 @@
         if target is to_core:
             twin[index].append(copy)
         return copy
+
+    storing = []
+
+    def stored():
+        for copy in storing:
+            copy.wait()
+        storing.clear()
 
     def own_copies(step):
         layer, which = step // 3, step % 3
@@ -614,14 +652,14 @@
                 target = out.at[pl.ds(pl.multiple_of(z * 1280 + i * 320, 8), 320), :]
             ins.append(pltpu.make_async_copy(source, copies.at[i], local))
             back.append(pltpu.make_async_copy(copies.at[i], target, local))
+        stored()
         for copy in ins:
             copy.start()
         for copy in ins:
             copy.wait()
         for copy in back:
             copy.start()
-        for copy in back:
-            copy.wait()
+        storing.extend(back)
 
     zed, mid, diag = {}, {}, {}
     zed[0] = start(0)
@@ -631,9 +669,11 @@
     for t in range(count + 2):
         if t < count:
             mid[t] = {}
-            for s in (1, 2, 3):
+            for s in (2, 3, 1):
                 for copy in zed[t][s - 1]:
                     copy.wait_recv()
+                if s == 2:
+                    pass_on(t)
                 mid[t][s] = (on(t, s, a, b, to_b), on(t, s, a, b, to_a))
                 on(t, s, a, b, to_core)
             if t + 2 < count:
@@ -658,6 +698,8 @@
                 on(k, s, 1 - a, 1 - b, to_core)
         if t + 1 < 3 * layers:
             own_copies(t + 1)
+        else:
+            stored()
         yield twin
 
 
@@ -714,10 +756,11 @@
     twin = next(ticks)
     clock = [-1]
     block = tokens.shape[1]
+    next(ticks)
     tokens_here = regroup(tokens, [context.at[pl.ds(step * block, block), :] for step in range(2)], 0)
     next(ticks)
     next(ticks)
-    clock[0] = 1
+    clock[0] = 2
     for copy in shared:
         copy.wait()
 
@@ -1481,7 +1524,9 @@
 ):
     z = lax.axis_index("shard")
     layers = attn_gain.shape[0]
-    rows = jnp.stack([attn_gain, attn_shift, query_bias, value_bias, out_bias, mlp_gain, mlp_shift, down_bias], axis=1)
+    rows = jnp.concatenate(
+        [attn_gain, attn_shift, query_bias, value_bias, out_bias, mlp_gain, mlp_shift, down_bias], axis=1
+    ).reshape(layers, 8, 320)
     part = jnp.zeros((layers, 24, 1280), BF16)
     part = lax.dynamic_update_slice(part, rows, (0, 0, z * 320))
     wide = lax.dynamic_update_slice(jnp.zeros((layers, 5120), BF16), up_bias, (0, z * 1280)).reshape(layers, 10, 512)

time: 879 us -> 852 us (0.969)
  Pallas kernels: 826 us -> 803 us
    pallas_call x1, Pallas kernels: 355 us -> 328 us  [forward_all(): pl.pallas_call(functools.partial(forward_kernel, layers), out_shape=out_s...]
where the time goes in v3:
time: 852 us; the launch traced here: 837 us
  Pallas kernels  803 us (94%)
  other arithmetic  23.7 us (3%)
  local copies, waits for them, and re-layouts  9.3 us (1%)
    pallas_call x1, Pallas kernels, backward_all(): pl.pallas_call(functools.partial(backward_kernel, layers), out_shape=out_...  475 us
    pallas_call x1, Pallas kernels, forward_all(): pl.pallas_call(functools.partial(forward_kernel, layers), out_shape=out_s...  328 us

profile of v3, /device:TPU:11, one launch (start us, length us, event | category | flops | bytes accessed | tf_op | source)
XLA Modules:
  0.0 836.7 jit_solution(16907392636890832169)
XLA Ops:
  0.7 0.7 convert_element_type.33
  1.3 0.7 broadcast_in_dim.14.refs_9_
  2.0 0.9 concatenate.6
  2.9 0.1 reshape.50
  3.0 0.7 constant_dynamic-update-slice_fusion
  3.7 1.2 dynamic_update_slice.9
  4.9 0.7 dynamic_update_slice.11.refs_8_
  5.6 0.0 copy-start.3
  5.6 0.6 copy-done.3
  6.2 327.6 %forward_all.1 = (bf16[2,4,1280,1280]{3,2,1,0:T(8,128)(2,1)}, bf16[2,1280,5120]{2,1,0:T(8,128)(2,1)}, bf16[2,5120,1280]{2,1,0:T(8,128)(2,1)}, bf16[2,1280,512]{2...) custom-call(bf16[2,256,1280]{2,1,0:T(8,128)(2,1)} %refs_0_.1, ...), custom_call_target="tpu_custom_call" | custom-call | tf_op jit(solution)/shard_map/forward_all/pallas_call | solution.py:959
  333.8 474.9 %backward_all.1 = (bf16[2,256,1280]{2,1,0:T(8,128)(2,1)}, bf16[2,256,1280]{2,1,0:T(8,128)(2,1)}, bf16[2,1280,1280]{2,1,0:T(8,128)(2,1)}, bf16[2,320,5120]{2,1,0:...) custom-call(bf16[2,256,1280]{2,1,0:T(8,128)(2,1)} %get-tuple-element, ...), custom_call_target="tpu_custom_call" | custom-call | tf_op jit(solution)/shard_map/backward_all/pallas_call | solution.py:1497
  808.8 0.0 copy-start.1
  808.8 1.0 slice.54
  809.8 0.9 fusion
  810.8 0.6 copy.41
  811.4 0.1 reshape_reshape.6
  811.6 0.6 slice_bitcast_fusion
  812.2 0.0 copy-start
  812.2 3.1 convert_element_type.34
  815.3 0.0 copy-done.1
  815.3 0.0 slice-start.2
  815.4 2.0 convert_element_type.41
  817.3 0.0 copy-done
  817.3 0.0 slice-start.3
  817.3 0.0 slice-start
  817.3 5.1 bitcast_convert_fusion
  822.5 0.0 slice-done.2
  822.5 0.0 slice-done.3
  822.5 0.0 slice-start.1
  822.5 6.8 convert_element_type.42
  829.2 0.0 slice-done
  829.2 0.0 slice-done.1
  829.2 0.0 copy-start.2
  829.2 6.0 convert_element_type.43
  835.2 0.0 copy-done.2
  835.2 1.1 copy.46
  (10 shorter events, 0.1 us)
Async XLA Ops:
  5.6 0.7 copy-start.3
  808.8 6.6 copy-start.1
  812.2 5.1 copy-start
  815.3 7.1 slice-start.2
  817.3 5.2 slice-start.3
  817.3 11.9 %slice-start = ((s8[6553600]{0:T(1024)(128)(4,1)}), s8[4194304]{0:T(1024)(128)(4,1)S(1)}, s32[]{:S(2)}) async-start(s8[6553600]{0:T(1024)(128)(4,1)} %bitcast.33), calls=%async_computation | async-start | bytes 8388608
  822.5 6.8 slice-start.1
  829.2 6.0 copy-start.2
